TPU v7x, 256 devices: a whole 4x4x8 slice. The times are simulated.
256 devices in a mesh: views: 4 (over z_hi, core), pages: 64 (over y, x, z_lo).
Axes of the slice: x: 4, y: 4, z: 8 (z_hi: 2, z_lo: 4; z = z_hi * 4 + z_lo), core: 2. Of those that a mesh axis runs over, the one named last changes fastest.
Arguments:
- weak_feats: bfloat16 [64, 8, 128, 512], P('pages', 'views'), may hold values from -6 to 6
- strong_feats: bfloat16 [64, 4, 8, 128, 256], P('pages', 'views'), may hold values from -6 to 6
- box_mask: int32 [64, 8, 128], P('pages'), may hold values 0 or 1
- teacher_weight: bfloat16 [512, 256], replicated, may hold values from -0.25 to 0.25
- head_one: bfloat16 [9, 256, 256], replicated, may hold values from -0.125 to 0.125
- head_two: bfloat16 [9, 256, 256], replicated, may hold values from -0.125 to 0.125
Outputs:
- grad_one: float32 [9, 256, 256], replicated
- grad_two: float32 [9, 256, 256], replicated
- mimic_loss: float32 [], replicated
All inputs are finite; a program needn't handle non-finite values. No bound on the sum of `box_mask` on one device may be relied on, other than what follows from the above.
Results may differ from a plain program's by a relative error of at most 0.0055.
Values may be sent and summed in bfloat16 or wider, within the bound.
No kernel may reach another device: no remote copies, remote signals or barrier semaphores. Data moves between devices by JAX's collectives and lax.ppermute only.
A program may use at most 64 MiB of HBM per device.

v0:
```python
import functools

import jax
import jax.numpy as jnp
import numpy as np
from jax import lax
from jax.experimental import pallas as pl
from jax.experimental.pallas import tpu as pltpu
from jax.sharding import Mesh, PartitionSpec as P

BF16 = jnp.bfloat16
F32 = jnp.float32
PLANE = ("zb", "x", "y")
FAR = ("zh", "za")
REACH = 2
TILE = 256
LANES = 128
TILES = 18
GRANT = 12 << 20
VMEM = pl.BlockSpec(memory_space=pltpu.VMEM)
SMEM = pl.BlockSpec(memory_space=pltpu.SMEM)
HBM = pl.BlockSpec(memory_space=pltpu.MemorySpace.HBM)
NOTE = 16


def call(body, outs, scratch, args, flops, specs=None, grant=GRANT):
    moved = sum(a.size * a.dtype.itemsize for a in args) + sum(
        int(np.prod(o.shape)) * o.dtype.itemsize for o in outs
    )
    return pl.pallas_call(
        body,
        out_shape=outs,
        in_specs=specs or [VMEM] * len(args),
        out_specs=[VMEM] * len(outs),
        scratch_shapes=scratch,
        compiler_params=pltpu.CompilerParams(vmem_limit_bytes=grant),
        cost_estimate=pl.CostEstimate(flops=flops, bytes_accessed=moved, transcendentals=0),
    )(*args)


def columns_moved(block, step):
    columns = block.shape[0]
    where = lax.broadcasted_iota(jnp.int32, block.shape, 0) + step
    rolled = pltpu.roll(block, (-step) % columns, 0)
    return jnp.where((where >= 0) & (where < columns), rolled, 0.0).astype(BF16)


def fill_shifts(pads, value_of, rows, columns, sign):
    edge = REACH * columns
    for j in range(3):
        zeros = jnp.zeros((edge, pads.shape[2]), BF16)
        pads[j, pl.ds(0, edge), :] = zeros
        pads[j, pl.ds(edge + rows * columns, edge), :] = zeros
    for r in range(rows):
        block = value_of(r)
        at = pl.ds(edge + r * columns, columns)
        pads[1, at, :] = block
        wide = block.astype(F32)
        pads[0, at, :] = columns_moved(wide, -sign * REACH)
        pads[2, at, :] = columns_moved(wide, sign * REACH)


def fill_turned(core, own_ref, give_ref, value_of, rows, columns):
    edge = REACH * columns
    half = own_ref.shape[0]
    for ref in (own_ref, give_ref):
        zeros = jnp.zeros((half, edge), BF16)
        ref[:, pl.ds(0, edge)] = zeros
        ref[:, pl.ds(edge + rows * columns, edge)] = zeros
    for r in range(rows):
        block = value_of(r).T
        at = pl.ds(edge + r * columns, columns)
        own_ref[:, at] = jnp.where(core == 0, block[:half], block[half:])
        give_ref[:, at] = jnp.where(core == 0, block[half:], block[:half])


def taps_at(pads, start, edge, sign):
    pieces = []
    for i in range(3):
        for j in range(3):
            row = start + (1 + sign * (i - 1)) * edge
            pieces.append(pads[j, pl.ds(pl.multiple_of(row, 128), TILE), :])
    return jnp.concatenate(pieces, axis=1)


def conv_rows(rows, columns, pads, k_ref, store):
    @pl.loop(0, rows * columns // TILE)
    def _(m):
        start = pl.multiple_of(m * TILE, TILE)
        store(
            pl.ds(start, TILE),
            jnp.dot(taps_at(pads, start, REACH * columns, 1), k_ref[...], preferred_element_type=F32),
        )


def teach_step(x_hbm, k_hbm, *refs):
    count = (len(refs) - 4) // 2
    sources, out_ref, targets = refs[:count], refs[count], refs[count + 1 : 2 * count + 1]
    x_ref, k_ref, sems = refs[-3:]
    pairs = [(x_hbm, x_ref), (k_hbm, k_ref), *zip(sources, targets)]
    loads = [pltpu.make_async_copy(*pair, sems.at[k]) for k, pair in enumerate(pairs)]
    for load in loads:
        load.start()
    for load in loads[:2]:
        load.wait()
    out_ref[...] = jnp.dot(x_ref[...], k_ref[...], preferred_element_type=F32).astype(BF16)
    for load in loads[2:]:
        load.wait()


def forward_step(
    rows, columns, place_ref, x_ref, one_ref, two_hbm,
    gate_ref, pred_ref, x_own, x_give, h_own, h_give, back_ref, pads, hidden, two_ref, sem,
):
    load = pltpu.make_async_copy(two_hbm, two_ref, sem)
    load.start()

    def of(ref):
        return lambda r: ref[pl.ds(r * columns, columns), :]

    def activate(at, total):
        hidden[at, :] = jnp.maximum(total, 0.0).astype(BF16)
        gate_ref[at, :] = jnp.where(total > 0, 1.0, 0.0).astype(BF16)

    def keep(at, total):
        pred_ref[at, :] = total

    core = place_ref[0] % 2
    channels = hidden.shape[1]
    fill_shifts(pads, of(x_ref), rows, columns, 1)
    conv_rows(rows, columns, pads, one_ref, activate)
    fill_turned(core, x_own, x_give, of(x_ref), rows, columns)
    fill_shifts(pads, of(hidden), rows, columns, 1)
    load.wait()
    conv_rows(rows, columns, pads, two_ref, keep)
    fill_turned(core, h_own, h_give, of(hidden), rows, columns)
    for k in range(9):
        at = pl.ds(k * channels, channels)
        back_ref[at, :] = two_ref[at, :].T


def terms(value):
    hi = value.astype(BF16).astype(F32)
    mid = (value - hi).astype(BF16).astype(F32)
    spot = lax.broadcasted_iota(jnp.int32, value.shape, 0)
    low = value - hi - mid
    return jnp.where(spot == 0, hi, jnp.where(spot == 1, mid, jnp.where(spot == 2, low, 0.0))).astype(BF16)


def mismatch_step(
    rows, columns, place_ref, pred_ref, own_ref, far_ref, near_ref, both_ref, box_ref,
    grad_ref, pads_ref,
):
    cells = rows * columns
    edge = REACH * columns
    per_view = rows // 4
    end, core = place_ref[0] // 2, place_ref[0] % 2
    losses = []
    for j in range(3):
        zeros = jnp.zeros((edge, pads_ref.shape[2]), BF16)
        pads_ref[j, pl.ds(0, edge), :] = zeros
        pads_ref[j, pl.ds(edge + cells, edge), :] = zeros
    views = ((own_ref, end, core), (near_ref, end, 1 - core), (far_ref, 1 - end, core), (both_ref, 1 - end, 1 - core))
    for block_ref, block_end, block_core in views:
        for q in range(per_view):
            r = (2 * block_end + block_core) * per_view + q
            start = pl.multiple_of(r * columns, columns)
            box = jnp.broadcast_to(box_ref[pl.ds(r, 1), :].astype(F32), (8, columns))
            weight = 1.0 + 3.0 * box.T[:, :1]
            gap = pred_ref[pl.ds(start, columns), :] - block_ref[pl.ds(q * columns, columns), :].astype(F32)
            scaled = weight * gap
            losses.append(jnp.sum(scaled * gap, axis=0, keepdims=True))
            value = (scaled / cells).astype(BF16)
            grad_ref[pl.ds(start, columns), :] = value
            wide = value.astype(F32)
            at = pl.ds(edge + start, columns)
            pads_ref[0, at, :] = columns_moved(wide, REACH)
            pads_ref[1, at, :] = value
            pads_ref[2, at, :] = columns_moved(wide, -REACH)
    loss = jnp.sum(functools.reduce(jnp.add, losses)) / (2.0 * cells)
    grad_ref[pl.ds(cells, NOTE), :] = terms(jnp.full((NOTE, grad_ref.shape[1]), loss, F32))


def back_step(rows, columns, pads_ref, k_ref, gate_ref, grad_ref):
    @pl.loop(0, rows * columns // TILE)
    def _(m):
        start = pl.multiple_of(m * TILE, TILE)
        total = jnp.dot(
            taps_at(pads_ref, start, REACH * columns, -1), k_ref[...], preferred_element_type=F32
        )
        at = pl.ds(start, TILE)
        grad_ref[at, :] = jnp.where(gate_ref[at, :].astype(F32) > 0, total, 0.0).astype(BF16)


def shifted_rows(out, value_of, rows, columns):
    for r in range(rows):
        block = value_of(r)
        wide = block.astype(F32)
        at = pl.ds(r * columns, columns)
        out[0, at, :] = columns_moved(wide, REACH)
        out[1, at, :] = block
        out[2, at, :] = columns_moved(wide, -REACH)


def pair_grad(rows, columns, turned, right, out_ref, base):
    cells, edge = rows * columns, REACH * columns
    half = turned[0].shape[0]
    left = jnp.concatenate(
        [jnp.concatenate([ref[:, pl.ds(i * edge, cells)] for ref in turned], axis=1) for i in range(3)],
        axis=0,
    )
    for j in range(3):
        grad = jnp.dot(left, right(j), preferred_element_type=F32).astype(BF16)
        for i in range(3):
            for row in range(half // 8):
                for side in range(grad.shape[1] // LANES):
                    d, t = divmod(side * 9 * half // 8 + (3 * i + j) * half // 8 + row, TILES)
                    out_ref[base + d, :, pl.ds(t * LANES, LANES)] = grad[
                        i * half + 8 * row : i * half + 8 * row + 8, side * LANES : (side + 1) * LANES
                    ]


def grad_two_step(rows, columns, own_turned, got_turned, pads_ref, got_ref, out_ref, moved):
    cells, edge = rows * columns, REACH * columns
    shifted_rows(moved, lambda r: got_ref[pl.ds(r * columns, columns), :], rows, columns)

    def right(j):
        return jnp.concatenate([pads_ref[j, pl.ds(edge, cells), :], moved[j]], axis=0)

    pair_grad(rows, columns, (own_turned, got_turned), right, out_ref, 0)


def grad_one_step(
    rows, columns, own_turned, got_turned, own_ref, got_ref, note_ref, other_note_ref, two_ref, out_ref, moved
):
    cells = rows * columns
    shifted_rows(moved.at[:, pl.ds(0, cells)], lambda r: own_ref[pl.ds(r * columns, columns), :], rows, columns)
    shifted_rows(moved.at[:, pl.ds(cells, cells)], lambda r: got_ref[pl.ds(r * columns, columns), :], rows, columns)
    share = two_ref.shape[0]
    pair_grad(rows, columns, (own_turned, got_turned), lambda j: moved[j], out_ref, share)
    at = (pl.ds(cells, NOTE), pl.ds(0, LANES))
    notes = note_ref[at].astype(F32) + other_note_ref[at].astype(F32)
    loss = jnp.sum(notes, axis=0, keepdims=True)
    tail = terms(jnp.broadcast_to(loss, (8, LANES)))
    for d in range(share):
        out_ref[d, :, pl.ds(0, TILES * LANES)] = two_ref[d]
    for d in range(2 * share):
        out_ref[d, :, pl.ds(TILES * LANES, LANES)] = tail


def place_half(slot, wide, ref, out_refs, sems):
    half = wide.shape[2]
    share = ref.shape[0] // 2
    copies = []
    for g in range(2):
        for k in range(9):
            for flat in range(9 * half // 8 * 2):
                side, row = divmod(flat, 9 * half // 8)
                if 8 * row // half == k:
                    d, t = divmod(flat, TILES)
                    wide[g, k, pl.ds(8 * row % half, 8), pl.ds(side * LANES, LANES)] = ref[
                        g * share + d, :, pl.ds(t * LANES, LANES)
                    ].astype(F32)
            copy = pltpu.make_async_copy(wide.at[g, k], out_refs[g].at[k, slot], sems.at[g, k])
            copy.start()
            copies.append(copy)
    for copy in copies:
        copy.wait()


def place_own(scale, place_ref, own_ref, total_ref, two_ref, one_ref, loss_ref, wide, sems):
    tail = total_ref[:, pl.ds(TILES * LANES, LANES)]
    spot = lax.broadcasted_iota(jnp.int32, tail.shape, 0)
    lane = lax.broadcasted_iota(jnp.int32, tail.shape, 1)
    loss_ref[0, 0] = jnp.sum(jnp.where((spot < 3) & (lane == 0), tail, 0.0)) * scale
    place_half(place_ref[0] % 2, wide, own_ref, (two_ref, one_ref), sems)


def place_other(place_ref, other_ref, two_in, one_in, two_ref, one_ref, wide, sems):
    place_half(1 - place_ref[0] % 2, wide, other_ref, (two_ref, one_ref), sems)


def in_place(value):
    return pltpu.with_memory_space_constraint(value, pltpu.MemorySpace.HBM)


def swap(value, axis):
    return lax.ppermute(value, axis, [(0, 1), (1, 0)])


def exchange(value, axes):
    return lax.all_to_all(value, axes, 0, 0, tiled=True)


def turn(value, step):
    count = lax.axis_size(FAR)
    return lax.ppermute(value, FAR, [(k, (k + step) % count) for k in range(count)])


def far_sum(value):
    two = turn(value, 2)
    one = turn(value, 1)
    three = turn(value, 3)
    return (value + two) + (one + three)


def placed(body, args, outs, in_specs, out_specs, aliases):
    return pl.pallas_call(
        body,
        out_shape=outs,
        in_specs=in_specs,
        out_specs=out_specs,
        scratch_shapes=[
            pltpu.VMEM((2, 9) + outs[0].shape[2:], F32),
            pltpu.SemaphoreType.DMA((2, 9)),
        ],
        input_output_aliases=aliases,
        compiler_params=pltpu.CompilerParams(vmem_limit_bytes=GRANT),
        cost_estimate=pl.CostEstimate(flops=0, bytes_accessed=6 * args[1].size, transcendentals=0),
    )(*args)


def per_device(weak_feats, strong_feats, box_mask, teacher_weight, head_one, head_two):
    channels = head_one.shape[2]
    in_channels = weak_feats.shape[3]
    rows, columns = strong_feats.shape[2:4]
    cells = rows * columns
    wide = (rows + 2 * REACH) * columns
    half = channels // 2
    shape = jax.ShapeDtypeStruct
    padded, plane, turned = (3, wide, channels), shape((cells, channels), BF16), shape((half, wide), BF16)
    kernel = (9 * channels, channels)
    flops = 2 * cells * 9 * channels * channels
    weak = in_place(weak_feats.reshape(-1, in_channels))
    teacher_weight = in_place(teacher_weight)
    operands = [in_place(strong_feats.reshape(cells, channels)), in_place(head_one.reshape(kernel))]
    last_kernel = in_place(head_two.reshape(kernel))
    own, *operands = call(
        teach_step,
        [shape((weak.shape[0], channels), BF16)] + [shape(a.shape, BF16) for a in operands],
        [pltpu.VMEM(weak.shape, BF16), pltpu.VMEM(teacher_weight.shape, BF16), pltpu.SemaphoreType.DMA((4,))],
        [weak, teacher_weight, *operands],
        2 * weak.size * channels,
        [HBM] * 4,
    )
    far = swap(own, "zh")
    where = (2 * lax.axis_index("zh") + lax.axis_index("c")).astype(jnp.int32).reshape(1)
    gate, prediction, x_own, x_give, h_own, h_give, back = call(
        functools.partial(forward_step, rows, columns),
        [plane, shape((cells, channels), F32)] + [turned] * 4 + [shape(kernel, BF16)],
        [
            pltpu.VMEM(padded, BF16),
            pltpu.VMEM((cells, channels), BF16),
            pltpu.VMEM(kernel, BF16),
            pltpu.SemaphoreType.DMA,
        ],
        [where, *operands, last_kernel],
        2 * flops,
        [SMEM, VMEM, VMEM, HBM],
    )
    own, x_give = lax.optimization_barrier((own, x_give))
    near, x_got, h_got = swap(own, "c"), swap(x_give, "c"), swap(h_give, "c")
    far, prediction, near, x_got, h_got = lax.optimization_barrier((far, prediction, near, x_got, h_got))
    both = swap(far, "c")
    grad, grad_pads = call(
        functools.partial(mismatch_step, rows, columns),
        [shape((cells + NOTE, channels), BF16), shape(padded, BF16)],
        [],
        [where, prediction, own, far, near, both, box_mask.reshape(rows, columns)],
        0,
        [SMEM] + [VMEM] * 6,
    )
    grad_got = swap(grad, "c")
    (pre,) = call(
        functools.partial(back_step, rows, columns),
        [plane],
        [],
        [grad_pads, back, gate],
        flops,
    )
    pre_got = swap(pre, "c")
    share = lax.axis_size(PLANE) // 2
    (two,) = call(
        functools.partial(grad_two_step, rows, columns),
        [shape((share, 8, TILES * LANES), BF16)],
        [pltpu.VMEM((3, cells, channels), BF16)],
        [h_own, h_got, grad_pads, grad_got],
        flops,
    )
    (message,) = call(
        functools.partial(grad_one_step, rows, columns),
        [shape((2 * share, 8, (TILES + 1) * LANES), BF16)],
        [pltpu.VMEM((3, 2 * cells, channels), BF16)],
        [x_own, x_got, pre, pre_got, grad, grad_got, two],
        flops,
    )
    total = far_sum(jnp.sum(exchange(message, PLANE).astype(F32), axis=0))
    piece = total[:, : TILES * LANES].astype(BF16)
    full = exchange(jnp.broadcast_to(piece[None], (2 * share,) + piece.shape), PLANE)
    other = swap(full, "c")
    loss_scale = 1.0 / (lax.axis_size(("zh", "c", "y", "x", "za", "zb")) * channels)
    parts = [shape((9, 2, half, channels), F32)] * 2
    two, one, loss = placed(
        functools.partial(place_own, loss_scale),
        [where, full, total],
        parts + [shape((1, 1), F32)],
        [SMEM, VMEM, VMEM],
        [HBM, HBM, SMEM],
        {},
    )
    other, two, one = lax.optimization_barrier((other, two, one))
    grad_two, grad_one = placed(
        place_other, [where, other, two, one], parts, [SMEM, VMEM, HBM, HBM], [HBM] * 2, {2: 0, 3: 1}
    )
    return (
        grad_one.reshape(9, channels, channels),
        grad_two.reshape(9, channels, channels),
        loss.reshape(()),
    )


def solution(mesh):
    split = Mesh(
        np.array(mesh.devices).reshape(2, 2, 4, 4, 2, 2), ("zh", "c", "y", "x", "za", "zb")
    )
    pages, views = ("y", "x", "za", "zb"), ("zh", "c")
    return jax.shard_map(
        per_device,
        mesh=split,
        in_specs=(
            P(pages, views, None, None),
            P(pages, views, None, None, None),
            P(pages, None, None),
            P(),
            P(),
            P(),
        ),
        out_specs=(P(), P(), P()),
        check_vma=False,
    )
```

profile of v0, /device:TPU:1, one launch (start us, length us, event | category | flops | bytes accessed | tf_op | source)
XLA Modules:
  0.0 98.3 jit_solution(4097216466150482948)
XLA Ops:
  0.6 1.6 %shard_map.85 = (bf16[256,256]{1,0:T(8,128)(2,1)S(1)}, bf16[1024,256]{1,0:T(8,128)(2,1)S(1)}, bf16[2304,256]{1,0:T(8,128)(2,1)S(1)}) custom-call(bf16[256,512]{1,0:T(8,128)(2,1)} %bitcast.14, bf16[512,256]{1,0:T(8,128)(2,1)} %k_hbm.1, bf16[1024,256]{1,0:T(8,128)(2,1)} %bitcast.13, bf16[2304,256]{1,0:T(8,128)(2,1)} %bitcast.12), custom_call_target="tpu_custom_call" | custom-call | flops 67108864 | bytes 4063232 | tf_op jit(solution)/shard_map/pallas_call | solution.py:30
  2.3 0.0 copy-start
  2.3 5.0 %shard_map.86 = (bf16[1024,256]{1,0:T(8,128)(2,1)S(1)}, f32[1024,256]{1,0:T(8,128)S(1)}, bf16[128,1536]{1,0:T(8,128)(2,1)S(1)}, bf16[128,1536]{1,0:T(8,128)(2,1)...) custom-call(s32[1]{0:T(128)} %bitcast.place_ref, ...), custom_call_target="tpu_custom_call" | custom-call | flops 2415919104 | bytes 7208964 | tf_op jit(solution)/shard_map/pallas_call | solution.py:30
  7.3 3.3 %collective-permute-start.2 = (bf16[128,1536]{1,0:T(8,128)(2,1)S(1)}, bf16[128,1536]{1,0:T(8,128)(2,1)S(1)}, u32[]{:S(2)}, u32[]{:S(2)}) collective-permute-start(bf16[128,1536]{1,0:T(8,128)(2,1)S(1)} %get-tuple-element.37), channel_id=1, source_target_pairs={{0,64},{64,0},{1,65},{65,1},{2,66},{66,2},{3,67},{67,3},{4,68},{68... | collective-permute-start | bytes 1179656 | tf_op jit(solution)/shard_map/ppermute | solution.py:288
  10.6 0.1 collective-permute-start.3
  10.7 5.2 %collective-permute-start = (bf16[256,256]{1,0:T(8,128)(2,1)S(1)}, bf16[256,256]{1,0:T(8,128)(2,1)S(1)}, u32[]{:S(2)}, u32[]{:S(2)}) collective-permute-start(bf16[256,256]{1,0:T(8,128)(2,1)S(1)} %get-tuple-element.36.own_ref), channel_id=1, source_target_pairs={{0,128},{128,0},{1,129},{129,1},{2,130},{130,2},{3,131},{131,3},{4... | collective-permute-start | bytes 393224 | tf_op jit(solution)/shard_map/ppermute | solution.py:288
  15.9 0.7 collective-permute-start.1
  16.6 2.6 %collective-permute-done.far_ref = bf16[256,256]{1,0:T(8,128)(2,1)S(1)} collective-permute-done((bf16[256,256]{1,0:T(8,128)(2,1)S(1)}, bf16[256,256]{1,0:T(8,128)(2,1)S(1)}, u32[]{:S(2)}, u32[]{:S(2)}) %collective-permute-start) | collective-permute-done | bytes 131104 | tf_op jit(solution)/shard_map/ppermute | solution.py:288
  19.2 0.0 collective-permute-done.1.near_ref
  19.2 0.0 collective-permute-done.2.got_turned
  19.2 0.0 collective-permute-done.3.got_turned
  19.3 1.5 %collective-permute-start.4 = (bf16[256,256]{1,0:T(8,128)(2,1)S(1)}, bf16[256,256]{1,0:T(8,128)(2,1)S(1)}, u32[]{:S(2)}, u32[]{:S(2)}) collective-permute-start(bf16[256,256]{1,0:T(8,128)(2,1)S(1)} %collective-permute-done.far_ref), channel_id=1, source_target_pairs={{0,64},{64,0},{1,65},{65,1},{2,66},{66,2},{3,67},{67,3},{4,68},{68... | collective-permute-start | bytes 393224 | tf_op jit(solution)/shard_map/ppermute | solution.py:288
  20.7 1.0 %collective-permute-done.4.both_ref = bf16[256,256]{1,0:T(8,128)(2,1)S(1)} collective-permute-done((bf16[256,256]{1,0:T(8,128)(2,1)S(1)}, bf16[256,256]{1,0:T(8,128)(2,1)S(1)}, u32[]{:S(2)}, u32[]{:S(2)}) %collective-permute-start.4) | collective-permute-done | bytes 131104 | tf_op jit(solution)/shard_map/ppermute | solution.py:288
  21.7 0.0 copy-done
  21.7 0.9 shard_map.87
  22.6 0.4 collective-permute-start.6
  23.0 1.9 %shard_map.88.own_ref = bf16[1024,256]{1,0:T(8,128)(2,1)S(1)} custom-call(bf16[3,1536,256]{2,1,0:T(8,128)(2,1)S(1)} %get-tuple-element.43.pads_ref, bf16[2304,256]{1,0:T(8,128)(2,1)S(1)} %get-tuple-element.44.k_ref, bf16[1024,256]{1,0:T(8,128)(2,1)S(1)} %get-tuple-element.45.gate_ref), custom_call_target="tpu_custom_call" | custom-call | flops 1207959552 | bytes 4587520 | tf_op jit(solution)/shard_map/pallas_call | solution.py:30
  24.9 0.2 collective-permute-start.5
  25.2 0.0 collective-permute-done.6.got_ref.other_note_ref
  25.2 1.4 %shard_map.89.two_ref = bf16[16,8,2304]{2,1,0:T(8,128)(2,1)S(1)} custom-call(bf16[128,1536]{1,0:T(8,128)(2,1)S(1)} %get-tuple-element.47.own_turned, bf16[128,1536]{1,0:T(8,128)(2,1)S(1)} %collective-permute-done.3.got_turned, bf16[3,1536,256]{2,1,0:T(8,128)(2,1)S(1)} %get-tuple-element.43.pads_ref, ...), custom_call_target="tpu_custom_call" | custom-call | flops 1207959552 | bytes 4268032 | tf_op jit(solution)/shard_map/pallas_call | solution.py:30
  26.6 0.4 collective-permute-done.5.got_ref
  26.9 1.4 %shard_map.90 = bf16[32,8,2432]{2,1,0:T(8,128)(2,1)S(1)} custom-call(bf16[128,1536]{1,0:T(8,128)(2,1)S(1)} %get-tuple-element.32.own_turned, bf16[128,1536]{1,0:T(8,128)(2,1)S(1)} %collective-permute-done.2.got_turned, bf16[1024,256]{1,0:T(8,128)(2,1)S(1)} %shard_map.88.own_ref, bf16[1024,256]{1,0:T(8,128)(2,1)S(1)} %collective-permute-done.5.got_ref, ...), custom_call_target="tpu_custom_call" | custom-call | flops 1207959552 | bytes 4734976 | tf_op jit(solution)/shard_map/pallas_call | solution.py:30
  28.4 28.7 %all_to_all.10 = bf16[32,8,2432]{2,1,0:T(8,128)(2,1)S(1)} all-to-all(bf16[32,8,2432]{2,1,0:T(8,128)(2,1)S(1)} %shard_map.90), channel_id=1, replica_groups=mesh['zh'=2,'c'=2,'y'=4,'x'=4,'za'=2,'zb'=2] {'zb','x','y'}, dimensions={0} | all-to-all | bytes 2490368 | tf_op jit(solution)/shard_map/all_to_all | solution.py:292
  57.1 0.2 convert_reduce_fusion
  57.2 4.0 %collective-permute-start.9 = (f32[8,2432]{1,0:T(8,128)S(1)}, f32[8,2432]{1,0:T(8,128)S(1)}, u32[]{:S(2)}, u32[]{:S(2)}) collective-permute-start(f32[8,2432]{1,0:T(8,128)S(1)} %convert_reduce_fusion), channel_id=1, source_target_pairs={{0,130},{2,0},{128,2},{130,128},{1,131},{3,1},{129,3},{131,129},{4... | collective-permute-start | bytes 233480 | tf_op jit(solution)/shard_map/ppermute | solution.py:297
  61.2 0.0 collective-permute-start.8
  61.2 3.8 %collective-permute-start.7 = (f32[8,2432]{1,0:T(8,128)S(1)}, f32[8,2432]{1,0:T(8,128)S(1)}, u32[]{:S(2)}, u32[]{:S(2)}) collective-permute-start(f32[8,2432]{1,0:T(8,128)S(1)} %convert_reduce_fusion), channel_id=1, source_target_pairs={{0,128},{2,130},{128,0},{130,2},{1,129},{3,131},{129,1},{131,3},{4... | collective-permute-start | bytes 233480 | tf_op jit(solution)/shard_map/ppermute | solution.py:297
  65.0 0.0 collective-permute-done.9
  65.0 1.8 %collective-permute-done.8 = f32[8,2432]{1,0:T(8,128)S(1)} collective-permute-done((f32[8,2432]{1,0:T(8,128)S(1)}, f32[8,2432]{1,0:T(8,128)S(1)}, u32[]{:S(2)}, u32[]{:S(2)}) %collective-permute-start.8) | collective-permute-done | bytes 77856 | tf_op jit(solution)/shard_map/ppermute | solution.py:297
  66.8 3.1 %collective-permute-done.7 = f32[8,2432]{1,0:T(8,128)S(1)} collective-permute-done((f32[8,2432]{1,0:T(8,128)S(1)}, f32[8,2432]{1,0:T(8,128)S(1)}, u32[]{:S(2)}, u32[]{:S(2)}) %collective-permute-start.7) | collective-permute-done | bytes 77856 | tf_op jit(solution)/shard_map/ppermute | solution.py:297
  69.9 0.1 broadcast_in_dim.2
  70.0 21.4 %all_to_all.11.own_ref = bf16[32,8,2304]{2,1,0:T(8,128)(2,1)S(1)} all-to-all(bf16[32,8,2304]{2,1,0:T(8,128)(2,1)S(1)} %broadcast_in_dim.2), channel_id=1, replica_groups=mesh['zh'=2,'c'=2,'y'=4,'x'=4,'za'=2,'zb'=2] {'zb','x','y'}, dimensions={0} | all-to-all | bytes 2359296 | tf_op jit(solution)/shard_map/all_to_all | solution.py:292
  91.4 2.9 %collective-permute-start.10 = (bf16[32,8,2304]{2,1,0:T(8,128)(2,1)S(1)}, bf16[32,8,2304]{2,1,0:T(8,128)(2,1)S(1)}, u32[]{:S(2)}, u32[]{:S(2)}) collective-permute-start(bf16[32,8,2304]{2,1,0:T(8,128)(2,1)S(1)} %all_to_all.11.own_ref), channel_id=1, source_target_pairs={{0,64},{64,0},{1,65},{65,1},{2,66},{66,2},{3,67},{67,3},{4,68},{68... | collective-permute-start | bytes 3538952 | tf_op jit(solution)/shard_map/ppermute | solution.py:288
  94.3 2.1 %shard_map.91 = (f32[9,2,128,256]{3,2,1,0:T(8,128)}, f32[9,2,128,256]{3,2,1,0:T(8,128)}, f32[1,1]{1,0:T(1,128)}) custom-call(s32[1]{0:T(128)} %bitcast.place_ref, bf16[32,8,2304]{2,1,0:T(8,128)(2,1)S(1)} %all_to_all.11.own_ref, f32[8,2432]{1,0:T(8,128)S(1)} %add_add_fusion.total_ref), custom_call_target="tpu_custom_call" | custom-call | bytes 3538944 | tf_op jit(solution)/shard_map/pallas_call | solution.py:308
  96.4 0.4 collective-permute-done.10.other_ref
  96.8 1.5 %shard_map.92 = (f32[9,2,128,256]{3,2,1,0:T(8,128)}, f32[9,2,128,256]{3,2,1,0:T(8,128)}) custom-call(s32[1]{0:T(128)} %bitcast.place_ref, bf16[32,8,2304]{2,1,0:T(8,128)(2,1)S(1)} %collective-permute-done.10.other_ref, f32[9,2,128,256]{3,2,1,0:T(8,128)} %get-tuple-element.52.two_in, ...), custom_call_target="tpu_custom_call", output_to_operand_aliasing={{0}: (2, {}), {1}: (3, {})} | custom-call | bytes 3538944 | tf_op jit(solution)/shard_map/pallas_call | solution.py:308
  (2 shorter events, 0.0 us)
Async XLA Ops:
  2.3 19.4 %copy-start = (s32[1,8,128]{2,1,0:T(8,128)S(1)}, s32[1,8,128]{2,1,0:T(8,128)}, u32[]{:S(2)}) copy-start(s32[1,8,128]{2,1,0:T(8,128)} %param.8) | copy-start | bytes 12292
  7.3 11.9 %collective-permute-start.2 = (bf16[128,1536]{1,0:T(8,128)(2,1)S(1)}, bf16[128,1536]{1,0:T(8,128)(2,1)S(1)}, u32[]{:S(2)}, u32[]{:S(2)}) collective-permute-start(bf16[128,1536]{1,0:T(8,128)(2,1)S(1)} %get-tuple-element.37), channel_id=1, source_target_pairs={{0,64},{64,0},{1,65},{65,1},{2,66},{66,2},{3,67},{67,3},{4,68},{68... | collective-permute-start | bytes 1179656 | tf_op jit(solution)/shard_map/ppermute | solution.py:288
  10.6 8.7 %collective-permute-start.3 = (bf16[128,1536]{1,0:T(8,128)(2,1)S(1)}, bf16[128,1536]{1,0:T(8,128)(2,1)S(1)}, u32[]{:S(2)}, u32[]{:S(2)}) collective-permute-start(bf16[128,1536]{1,0:T(8,128)(2,1)S(1)} %get-tuple-element.38), channel_id=1, source_target_pairs={{0,64},{64,0},{1,65},{65,1},{2,66},{66,2},{3,67},{67,3},{4,68},{68... | collective-permute-start | bytes 1179656 | tf_op jit(solution)/shard_map/ppermute | solution.py:288
  10.7 8.6 %collective-permute-start = (bf16[256,256]{1,0:T(8,128)(2,1)S(1)}, bf16[256,256]{1,0:T(8,128)(2,1)S(1)}, u32[]{:S(2)}, u32[]{:S(2)}) collective-permute-start(bf16[256,256]{1,0:T(8,128)(2,1)S(1)} %get-tuple-element.36.own_ref), channel_id=1, source_target_pairs={{0,128},{128,0},{1,129},{129,1},{2,130},{130,2},{3,131},{131,3},{4... | collective-permute-start | bytes 393224 | tf_op jit(solution)/shard_map/ppermute | solution.py:288
  15.9 3.3 %collective-permute-start.1 = (bf16[256,256]{1,0:T(8,128)(2,1)S(1)}, bf16[256,256]{1,0:T(8,128)(2,1)S(1)}, u32[]{:S(2)}, u32[]{:S(2)}) collective-permute-start(bf16[256,256]{1,0:T(8,128)(2,1)S(1)} %get-tuple-element.36.own_ref), channel_id=1, source_target_pairs={{0,64},{64,0},{1,65},{65,1},{2,66},{66,2},{3,67},{67,3},{4,68},{68... | collective-permute-start | bytes 393224 | tf_op jit(solution)/shard_map/ppermute | solution.py:288
  19.3 2.4 %collective-permute-start.4 = (bf16[256,256]{1,0:T(8,128)(2,1)S(1)}, bf16[256,256]{1,0:T(8,128)(2,1)S(1)}, u32[]{:S(2)}, u32[]{:S(2)}) collective-permute-start(bf16[256,256]{1,0:T(8,128)(2,1)S(1)} %collective-permute-done.far_ref), channel_id=1, source_target_pairs={{0,64},{64,0},{1,65},{65,1},{2,66},{66,2},{3,67},{67,3},{4,68},{68... | collective-permute-start | bytes 393224 | tf_op jit(solution)/shard_map/ppermute | solution.py:288
  22.6 2.6 %collective-permute-start.6 = (bf16[1040,256]{1,0:T(8,128)(2,1)S(1)}, bf16[1040,256]{1,0:T(8,128)(2,1)S(1)}, u32[]{:S(2)}, u32[]{:S(2)}) collective-permute-start(bf16[1040,256]{1,0:T(8,128)(2,1)S(1)} %get-tuple-element.46.note_ref), channel_id=1, source_target_pairs={{0,64},{64,0},{1,65},{65,1},{2,66},{66,2},{3,67},{67,3},{4,68},{68... | collective-permute-start | bytes 1597448 | tf_op jit(solution)/shard_map/ppermute | solution.py:288
  24.9 2.0 %collective-permute-start.5 = (bf16[1024,256]{1,0:T(8,128)(2,1)S(1)}, bf16[1024,256]{1,0:T(8,128)(2,1)S(1)}, u32[]{:S(2)}, u32[]{:S(2)}) collective-permute-start(bf16[1024,256]{1,0:T(8,128)(2,1)S(1)} %shard_map.88.own_ref), channel_id=1, source_target_pairs={{0,64},{64,0},{1,65},{65,1},{2,66},{66,2},{3,67},{67,3},{4,68},{68... | collective-permute-start | bytes 1572872 | tf_op jit(solution)/shard_map/ppermute | solution.py:288
  57.2 7.8 %collective-permute-start.9 = (f32[8,2432]{1,0:T(8,128)S(1)}, f32[8,2432]{1,0:T(8,128)S(1)}, u32[]{:S(2)}, u32[]{:S(2)}) collective-permute-start(f32[8,2432]{1,0:T(8,128)S(1)} %convert_reduce_fusion), channel_id=1, source_target_pairs={{0,130},{2,0},{128,2},{130,128},{1,131},{3,1},{129,3},{131,129},{4... | collective-permute-start | bytes 233480 | tf_op jit(solution)/shard_map/ppermute | solution.py:297
  61.2 5.6 %collective-permute-start.8 = (f32[8,2432]{1,0:T(8,128)S(1)}, f32[8,2432]{1,0:T(8,128)S(1)}, u32[]{:S(2)}, u32[]{:S(2)}) collective-permute-start(f32[8,2432]{1,0:T(8,128)S(1)} %convert_reduce_fusion), channel_id=1, source_target_pairs={{0,2},{2,128},{128,130},{130,0},{1,3},{3,129},{129,131},{131,1},{4... | collective-permute-start | bytes 233480 | tf_op jit(solution)/shard_map/ppermute | solution.py:297
  61.2 8.7 %collective-permute-start.7 = (f32[8,2432]{1,0:T(8,128)S(1)}, f32[8,2432]{1,0:T(8,128)S(1)}, u32[]{:S(2)}, u32[]{:S(2)}) collective-permute-start(f32[8,2432]{1,0:T(8,128)S(1)} %convert_reduce_fusion), channel_id=1, source_target_pairs={{0,128},{2,130},{128,0},{130,2},{1,129},{3,131},{129,1},{131,3},{4... | collective-permute-start | bytes 233480 | tf_op jit(solution)/shard_map/ppermute | solution.py:297
  91.4 5.4 %collective-permute-start.10 = (bf16[32,8,2304]{2,1,0:T(8,128)(2,1)S(1)}, bf16[32,8,2304]{2,1,0:T(8,128)(2,1)S(1)}, u32[]{:S(2)}, u32[]{:S(2)}) collective-permute-start(bf16[32,8,2304]{2,1,0:T(8,128)(2,1)S(1)} %all_to_all.11.own_ref), channel_id=1, source_target_pairs={{0,64},{64,0},{1,65},{65,1},{2,66},{66,2},{3,67},{67,3},{4,68},{68... | collective-permute-start | bytes 3538952 | tf_op jit(solution)/shard_map/ppermute | solution.py:288
where the time goes:
time: 98.5 us; the launch traced here: 98.3 us
  blocking collectives  50.1 us (51%)
  starting transfers between devices  22.1 us (22%)
  Pallas kernels  15.9 us (16%)
  waiting for transfers between devices  9.27 us (9%)
    all_to_all x2, blocking collectives, exchange(): return lax.all_to_all(value, axes, 0, 0, tiled=True)  50.1 us
    ppermute x8, starting transfers between devices, swap(): return lax.ppermute(value, axis, [(0, 1), (1, 0)])  14.3 us
    pallas_call x6, Pallas kernels, call(): pl.pallas_call(body, out_shape=outs, in_specs=specs or [VMEM] * len(args)...  12.2 us
    ppermute x3, starting transfers between devices, turn(): lax.ppermute(value, FAR, [(k, (k + step) % count) for k in range(count)])  7.77 us
    ppermute x3, waiting for transfers between devices, turn(): lax.ppermute(value, FAR, [(k, (k + step) % count) for k in range(count)])  4.86 us
    ppermute x8, waiting for transfers between devices, swap(): return lax.ppermute(value, axis, [(0, 1), (1, 0)])  4.41 us
    pallas_call x2, Pallas kernels, placed(): pl.pallas_call(body, out_shape=outs, in_specs=in_specs, out_specs=out_spe...  3.61 us
  transfers between devices with their start and end apart: 11, of which 6 were waited for; matrix products, arithmetic and copies ran while one was open for 0% of the time, Pallas kernels for 5%

commit v1 on v0

--- a/solution.py
+++ b/solution.py
@@ -13,7 +13,8 @@
 PLANE = ("zb", "x", "y")
 FAR = ("zh", "za")
 REACH = 2
-TILE = 256
+TILE = 512
+BACK_TILE = 1024
 LANES = 128
 TILES = 18
 GRANT = 12 << 20
@@ -74,12 +75,12 @@
         give_ref[:, at] = jnp.where(core == 0, block[half:], block[:half])
 
 
-def taps_at(pads, start, edge, sign):
+def taps_at(pads, start, size, edge, sign):
     pieces = []
     for i in range(3):
         for j in range(3):
             row = start + (1 + sign * (i - 1)) * edge
-            pieces.append(pads[j, pl.ds(pl.multiple_of(row, 128), TILE), :])
+            pieces.append(pads[j, pl.ds(pl.multiple_of(row, 128), size), :])
     return jnp.concatenate(pieces, axis=1)
 
 
@@ -89,7 +90,7 @@
         start = pl.multiple_of(m * TILE, TILE)
         store(
             pl.ds(start, TILE),
-            jnp.dot(taps_at(pads, start, REACH * columns, 1), k_ref[...], preferred_element_type=F32),
+            jnp.dot(taps_at(pads, start, TILE, REACH * columns, 1), k_ref[...], preferred_element_type=F32),
         )
 
 
@@ -182,13 +183,13 @@
 
 
 def back_step(rows, columns, pads_ref, k_ref, gate_ref, grad_ref):
-    @pl.loop(0, rows * columns // TILE)
+    @pl.loop(0, rows * columns // BACK_TILE)
     def _(m):
-        start = pl.multiple_of(m * TILE, TILE)
+        start = pl.multiple_of(m * BACK_TILE, BACK_TILE)
         total = jnp.dot(
-            taps_at(pads_ref, start, REACH * columns, -1), k_ref[...], preferred_element_type=F32
+            taps_at(pads_ref, start, BACK_TILE, REACH * columns, -1), k_ref[...], preferred_element_type=F32
         )
-        at = pl.ds(start, TILE)
+        at = pl.ds(start, BACK_TILE)
         grad_ref[at, :] = jnp.where(gate_ref[at, :].astype(F32) > 0, total, 0.0).astype(BF16)
 
 

time: 98.5 us -> 96.6 us (0.981)
  the two profiles are of different devices: /device:TPU:1 before, /device:TPU:97 now
where the time goes in v1:
time: 96.6 us; the launch traced here: 95.1 us
  blocking collectives  51.4 us (53%)
  starting transfers between devices  19.3 us (20%)
  Pallas kernels  14.6 us (15%)
  waiting for transfers between devices  8.76 us (9%)
    all_to_all x2, blocking collectives, exchange(): return lax.all_to_all(value, axes, 0, 0, tiled=True)  51.4 us
    pallas_call x6, Pallas kernels, call(): pl.pallas_call(body, out_shape=outs, in_specs=specs or [VMEM] * len(args)...  11 us
    ppermute x8, starting transfers between devices, swap(): return lax.ppermute(value, axis, [(0, 1), (1, 0)])  10.8 us
    ppermute x3, starting transfers between devices, turn(): lax.ppermute(value, FAR, [(k, (k + step) % count) for k in range(count)])  8.51 us
    ppermute x8, waiting for transfers between devices, swap(): return lax.ppermute(value, axis, [(0, 1), (1, 0)])  5.41 us
    pallas_call x2, Pallas kernels, placed(): pl.pallas_call(body, out_shape=outs, in_specs=in_specs, out_specs=out_spe...  3.61 us
    ppermute x3, waiting for transfers between devices, turn(): lax.ppermute(value, FAR, [(k, (k + step) % count) for k in range(count)])  3.35 us
  transfers between devices with their start and end apart: 11, of which 5 were waited for; matrix products, arithmetic and copies ran while one was open for 0% of the time, Pallas kernels for 5%

profile of v1, /device:TPU:97, one launch (start us, length us, event | category | flops | bytes accessed | tf_op | source)
XLA Modules:
  0.0 95.1 jit_solution(4541956390209103198)
XLA Ops:
  0.6 1.6 %shard_map.85 = (bf16[256,256]{1,0:T(8,128)(2,1)S(1)}, bf16[1024,256]{1,0:T(8,128)(2,1)S(1)}, bf16[2304,256]{1,0:T(8,128)(2,1)S(1)}) custom-call(bf16[256,512]{1,0:T(8,128)(2,1)} %bitcast.14, bf16[512,256]{1,0:T(8,128)(2,1)} %k_hbm.1, bf16[1024,256]{1,0:T(8,128)(2,1)} %bitcast.13, bf16[2304,256]{1,0:T(8,128)(2,1)} %bitcast.12), custom_call_target="tpu_custom_call" | custom-call | flops 67108864 | bytes 4063232 | tf_op jit(solution)/shard_map/pallas_call | solution.py:31
  2.3 0.0 copy-start
  2.3 4.3 %shard_map.86 = (bf16[1024,256]{1,0:T(8,128)(2,1)S(1)}, f32[1024,256]{1,0:T(8,128)S(1)}, bf16[128,1536]{1,0:T(8,128)(2,1)S(1)}, bf16[128,1536]{1,0:T(8,128)(2,1)...) custom-call(s32[1]{0:T(128)} %bitcast.place_ref, ...), custom_call_target="tpu_custom_call" | custom-call | flops 2415919104 | bytes 7208964 | tf_op jit(solution)/shard_map/pallas_call | solution.py:31
  6.6 0.8 collective-permute-start.2
  7.3 0.1 collective-permute-start.3
  7.4 4.2 %collective-permute-start = (bf16[256,256]{1,0:T(8,128)(2,1)S(1)}, bf16[256,256]{1,0:T(8,128)(2,1)S(1)}, u32[]{:S(2)}, u32[]{:S(2)}) collective-permute-start(bf16[256,256]{1,0:T(8,128)(2,1)S(1)} %get-tuple-element.36.own_ref), channel_id=1, source_target_pairs={{0,128},{128,0},{1,129},{129,1},{2,130},{130,2},{3,131},{131,3},{4... | collective-permute-start | bytes 393224 | tf_op jit(solution)/shard_map/ppermute | solution.py:289
  11.6 0.7 collective-permute-start.1
  12.3 3.6 %collective-permute-done.far_ref = bf16[256,256]{1,0:T(8,128)(2,1)S(1)} collective-permute-done((bf16[256,256]{1,0:T(8,128)(2,1)S(1)}, bf16[256,256]{1,0:T(8,128)(2,1)S(1)}, u32[]{:S(2)}, u32[]{:S(2)}) %collective-permute-start) | collective-permute-done | bytes 131104 | tf_op jit(solution)/shard_map/ppermute | solution.py:289
  16.0 0.0 collective-permute-done.1.near_ref
  16.0 0.0 collective-permute-done.2.got_turned
  16.0 0.0 collective-permute-done.3.got_turned
  16.0 1.5 %collective-permute-start.4 = (bf16[256,256]{1,0:T(8,128)(2,1)S(1)}, bf16[256,256]{1,0:T(8,128)(2,1)S(1)}, u32[]{:S(2)}, u32[]{:S(2)}) collective-permute-start(bf16[256,256]{1,0:T(8,128)(2,1)S(1)} %collective-permute-done.far_ref), channel_id=1, source_target_pairs={{0,64},{64,0},{1,65},{65,1},{2,66},{66,2},{3,67},{67,3},{4,68},{68... | collective-permute-start | bytes 393224 | tf_op jit(solution)/shard_map/ppermute | solution.py:289
  17.5 1.0 %collective-permute-done.4.both_ref = bf16[256,256]{1,0:T(8,128)(2,1)S(1)} collective-permute-done((bf16[256,256]{1,0:T(8,128)(2,1)S(1)}, bf16[256,256]{1,0:T(8,128)(2,1)S(1)}, u32[]{:S(2)}, u32[]{:S(2)}) %collective-permute-start.4) | collective-permute-done | bytes 131104 | tf_op jit(solution)/shard_map/ppermute | solution.py:289
  18.4 0.0 copy-done
  18.4 0.9 shard_map.87
  19.3 0.4 collective-permute-start.6
  19.8 1.4 %shard_map.88.own_ref = bf16[1024,256]{1,0:T(8,128)(2,1)S(1)} custom-call(bf16[3,1536,256]{2,1,0:T(8,128)(2,1)S(1)} %get-tuple-element.43.pads_ref, bf16[2304,256]{1,0:T(8,128)(2,1)S(1)} %get-tuple-element.44.k_ref, bf16[1024,256]{1,0:T(8,128)(2,1)S(1)} %get-tuple-element.45.gate_ref), custom_call_target="tpu_custom_call" | custom-call | flops 1207959552 | bytes 4587520 | tf_op jit(solution)/shard_map/pallas_call | solution.py:31
  21.2 0.2 collective-permute-start.5
  21.4 0.0 collective-permute-done.6.got_ref.other_note_ref
  21.4 1.4 %shard_map.89.two_ref = bf16[16,8,2304]{2,1,0:T(8,128)(2,1)S(1)} custom-call(bf16[128,1536]{1,0:T(8,128)(2,1)S(1)} %get-tuple-element.47.own_turned, bf16[128,1536]{1,0:T(8,128)(2,1)S(1)} %collective-permute-done.3.got_turned, bf16[3,1536,256]{2,1,0:T(8,128)(2,1)S(1)} %get-tuple-element.43.pads_ref, ...), custom_call_target="tpu_custom_call" | custom-call | flops 1207959552 | bytes 4268032 | tf_op jit(solution)/shard_map/pallas_call | solution.py:31
  22.8 0.4 collective-permute-done.5.got_ref
  23.2 1.4 %shard_map.90 = bf16[32,8,2432]{2,1,0:T(8,128)(2,1)S(1)} custom-call(bf16[128,1536]{1,0:T(8,128)(2,1)S(1)} %get-tuple-element.32.own_turned, bf16[128,1536]{1,0:T(8,128)(2,1)S(1)} %collective-permute-done.2.got_turned, bf16[1024,256]{1,0:T(8,128)(2,1)S(1)} %shard_map.88.own_ref, bf16[1024,256]{1,0:T(8,128)(2,1)S(1)} %collective-permute-done.5.got_ref, ...), custom_call_target="tpu_custom_call" | custom-call | flops 1207959552 | bytes 4734976 | tf_op jit(solution)/shard_map/pallas_call | solution.py:31
  24.6 27.9 %all_to_all.10 = bf16[32,8,2432]{2,1,0:T(8,128)(2,1)S(1)} all-to-all(bf16[32,8,2432]{2,1,0:T(8,128)(2,1)S(1)} %shard_map.90), channel_id=1, replica_groups=mesh['zh'=2,'c'=2,'y'=4,'x'=4,'za'=2,'zb'=2] {'zb','x','y'}, dimensions={0} | all-to-all | bytes 2490368 | tf_op jit(solution)/shard_map/all_to_all | solution.py:293
  52.5 0.2 convert_reduce_fusion
  52.7 1.3 %collective-permute-start.9 = (f32[8,2432]{1,0:T(8,128)S(1)}, f32[8,2432]{1,0:T(8,128)S(1)}, u32[]{:S(2)}, u32[]{:S(2)}) collective-permute-start(f32[8,2432]{1,0:T(8,128)S(1)} %convert_reduce_fusion), channel_id=1, source_target_pairs={{0,130},{2,0},{128,2},{130,128},{1,131},{3,1},{129,3},{131,129},{4... | collective-permute-start | bytes 233480 | tf_op jit(solution)/shard_map/ppermute | solution.py:298
  54.0 3.3 %collective-permute-start.8 = (f32[8,2432]{1,0:T(8,128)S(1)}, f32[8,2432]{1,0:T(8,128)S(1)}, u32[]{:S(2)}, u32[]{:S(2)}) collective-permute-start(f32[8,2432]{1,0:T(8,128)S(1)} %convert_reduce_fusion), channel_id=1, source_target_pairs={{0,2},{2,128},{128,130},{130,0},{1,3},{3,129},{129,131},{131,1},{4... | collective-permute-start | bytes 233480 | tf_op jit(solution)/shard_map/ppermute | solution.py:298
  57.3 3.8 %collective-permute-start.7 = (f32[8,2432]{1,0:T(8,128)S(1)}, f32[8,2432]{1,0:T(8,128)S(1)}, u32[]{:S(2)}, u32[]{:S(2)}) collective-permute-start(f32[8,2432]{1,0:T(8,128)S(1)} %convert_reduce_fusion), channel_id=1, source_target_pairs={{0,128},{2,130},{128,0},{130,2},{1,129},{3,131},{129,1},{131,3},{4... | collective-permute-start | bytes 233480 | tf_op jit(solution)/shard_map/ppermute | solution.py:298
  61.2 0.0 collective-permute-done.9
  61.2 0.0 collective-permute-done.8
  61.2 3.3 %collective-permute-done.7 = f32[8,2432]{1,0:T(8,128)S(1)} collective-permute-done((f32[8,2432]{1,0:T(8,128)S(1)}, f32[8,2432]{1,0:T(8,128)S(1)}, u32[]{:S(2)}, u32[]{:S(2)}) %collective-permute-start.7) | collective-permute-done | bytes 77856 | tf_op jit(solution)/shard_map/ppermute | solution.py:298
  64.6 0.1 broadcast_in_dim.2
  64.7 23.5 %all_to_all.11.own_ref = bf16[32,8,2304]{2,1,0:T(8,128)(2,1)S(1)} all-to-all(bf16[32,8,2304]{2,1,0:T(8,128)(2,1)S(1)} %broadcast_in_dim.2), channel_id=1, replica_groups=mesh['zh'=2,'c'=2,'y'=4,'x'=4,'za'=2,'zb'=2] {'zb','x','y'}, dimensions={0} | all-to-all | bytes 2359296 | tf_op jit(solution)/shard_map/all_to_all | solution.py:293
  88.2 2.9 %collective-permute-start.10 = (bf16[32,8,2304]{2,1,0:T(8,128)(2,1)S(1)}, bf16[32,8,2304]{2,1,0:T(8,128)(2,1)S(1)}, u32[]{:S(2)}, u32[]{:S(2)}) collective-permute-start(bf16[32,8,2304]{2,1,0:T(8,128)(2,1)S(1)} %all_to_all.11.own_ref), channel_id=1, source_target_pairs={{0,64},{64,0},{1,65},{65,1},{2,66},{66,2},{3,67},{67,3},{4,68},{68... | collective-permute-start | bytes 3538952 | tf_op jit(solution)/shard_map/ppermute | solution.py:289
  91.1 2.1 %shard_map.91 = (f32[9,2,128,256]{3,2,1,0:T(8,128)}, f32[9,2,128,256]{3,2,1,0:T(8,128)}, f32[1,1]{1,0:T(1,128)}) custom-call(s32[1]{0:T(128)} %bitcast.place_ref, bf16[32,8,2304]{2,1,0:T(8,128)(2,1)S(1)} %all_to_all.11.own_ref, f32[8,2432]{1,0:T(8,128)S(1)} %add_add_fusion.total_ref), custom_call_target="tpu_custom_call" | custom-call | bytes 3538944 | tf_op jit(solution)/shard_map/pallas_call | solution.py:309
  93.2 0.4 collective-permute-done.10.other_ref
  93.6 1.5 %shard_map.92 = (f32[9,2,128,256]{3,2,1,0:T(8,128)}, f32[9,2,128,256]{3,2,1,0:T(8,128)}) custom-call(s32[1]{0:T(128)} %bitcast.place_ref, bf16[32,8,2304]{2,1,0:T(8,128)(2,1)S(1)} %collective-permute-done.10.other_ref, f32[9,2,128,256]{3,2,1,0:T(8,128)} %get-tuple-element.52.two_in, ...), custom_call_target="tpu_custom_call", output_to_operand_aliasing={{0}: (2, {}), {1}: (3, {})} | custom-call | bytes 3538944 | tf_op jit(solution)/shard_map/pallas_call | solution.py:309
  (2 shorter events, 0.0 us)
Async XLA Ops:
  2.3 16.2 %copy-start = (s32[1,8,128]{2,1,0:T(8,128)S(1)}, s32[1,8,128]{2,1,0:T(8,128)}, u32[]{:S(2)}) copy-start(s32[1,8,128]{2,1,0:T(8,128)} %param.8) | copy-start | bytes 12292
  6.6 9.4 %collective-permute-start.2 = (bf16[128,1536]{1,0:T(8,128)(2,1)S(1)}, bf16[128,1536]{1,0:T(8,128)(2,1)S(1)}, u32[]{:S(2)}, u32[]{:S(2)}) collective-permute-start(bf16[128,1536]{1,0:T(8,128)(2,1)S(1)} %get-tuple-element.37), channel_id=1, source_target_pairs={{0,64},{64,0},{1,65},{65,1},{2,66},{66,2},{3,67},{67,3},{4,68},{68... | collective-permute-start | bytes 1179656 | tf_op jit(solution)/shard_map/ppermute | solution.py:289
  7.3 8.7 %collective-permute-start.3 = (bf16[128,1536]{1,0:T(8,128)(2,1)S(1)}, bf16[128,1536]{1,0:T(8,128)(2,1)S(1)}, u32[]{:S(2)}, u32[]{:S(2)}) collective-permute-start(bf16[128,1536]{1,0:T(8,128)(2,1)S(1)} %get-tuple-element.38), channel_id=1, source_target_pairs={{0,64},{64,0},{1,65},{65,1},{2,66},{66,2},{3,67},{67,3},{4,68},{68... | collective-permute-start | bytes 1179656 | tf_op jit(solution)/shard_map/ppermute | solution.py:289
  7.4 8.6 %collective-permute-start = (bf16[256,256]{1,0:T(8,128)(2,1)S(1)}, bf16[256,256]{1,0:T(8,128)(2,1)S(1)}, u32[]{:S(2)}, u32[]{:S(2)}) collective-permute-start(bf16[256,256]{1,0:T(8,128)(2,1)S(1)} %get-tuple-element.36.own_ref), channel_id=1, source_target_pairs={{0,128},{128,0},{1,129},{129,1},{2,130},{130,2},{3,131},{131,3},{4... | collective-permute-start | bytes 393224 | tf_op jit(solution)/shard_map/ppermute | solution.py:289
  11.6 4.3 %collective-permute-start.1 = (bf16[256,256]{1,0:T(8,128)(2,1)S(1)}, bf16[256,256]{1,0:T(8,128)(2,1)S(1)}, u32[]{:S(2)}, u32[]{:S(2)}) collective-permute-start(bf16[256,256]{1,0:T(8,128)(2,1)S(1)} %get-tuple-element.36.own_ref), channel_id=1, source_target_pairs={{0,64},{64,0},{1,65},{65,1},{2,66},{66,2},{3,67},{67,3},{4,68},{68... | collective-permute-start | bytes 393224 | tf_op jit(solution)/shard_map/ppermute | solution.py:289
  16.0 2.4 %collective-permute-start.4 = (bf16[256,256]{1,0:T(8,128)(2,1)S(1)}, bf16[256,256]{1,0:T(8,128)(2,1)S(1)}, u32[]{:S(2)}, u32[]{:S(2)}) collective-permute-start(bf16[256,256]{1,0:T(8,128)(2,1)S(1)} %collective-permute-done.far_ref), channel_id=1, source_target_pairs={{0,64},{64,0},{1,65},{65,1},{2,66},{66,2},{3,67},{67,3},{4,68},{68... | collective-permute-start | bytes 393224 | tf_op jit(solution)/shard_map/ppermute | solution.py:289
  19.3 2.1 %collective-permute-start.6 = (bf16[1040,256]{1,0:T(8,128)(2,1)S(1)}, bf16[1040,256]{1,0:T(8,128)(2,1)S(1)}, u32[]{:S(2)}, u32[]{:S(2)}) collective-permute-start(bf16[1040,256]{1,0:T(8,128)(2,1)S(1)} %get-tuple-element.46.note_ref), channel_id=1, source_target_pairs={{0,64},{64,0},{1,65},{65,1},{2,66},{66,2},{3,67},{67,3},{4,68},{68... | collective-permute-start | bytes 1597448 | tf_op jit(solution)/shard_map/ppermute | solution.py:289
  21.2 2.0 %collective-permute-start.5 = (bf16[1024,256]{1,0:T(8,128)(2,1)S(1)}, bf16[1024,256]{1,0:T(8,128)(2,1)S(1)}, u32[]{:S(2)}, u32[]{:S(2)}) collective-permute-start(bf16[1024,256]{1,0:T(8,128)(2,1)S(1)} %shard_map.88.own_ref), channel_id=1, source_target_pairs={{0,64},{64,0},{1,65},{65,1},{2,66},{66,2},{3,67},{67,3},{4,68},{68... | collective-permute-start | bytes 1572872 | tf_op jit(solution)/shard_map/ppermute | solution.py:289
  52.7 8.5 %collective-permute-start.9 = (f32[8,2432]{1,0:T(8,128)S(1)}, f32[8,2432]{1,0:T(8,128)S(1)}, u32[]{:S(2)}, u32[]{:S(2)}) collective-permute-start(f32[8,2432]{1,0:T(8,128)S(1)} %convert_reduce_fusion), channel_id=1, source_target_pairs={{0,130},{2,0},{128,2},{130,128},{1,131},{3,1},{129,3},{131,129},{4... | collective-permute-start | bytes 233480 | tf_op jit(solution)/shard_map/ppermute | solution.py:298
  54.0 7.2 %collective-permute-start.8 = (f32[8,2432]{1,0:T(8,128)S(1)}, f32[8,2432]{1,0:T(8,128)S(1)}, u32[]{:S(2)}, u32[]{:S(2)}) collective-permute-start(f32[8,2432]{1,0:T(8,128)S(1)} %convert_reduce_fusion), channel_id=1, source_target_pairs={{0,2},{2,128},{128,130},{130,0},{1,3},{3,129},{129,131},{131,1},{4... | collective-permute-start | bytes 233480 | tf_op jit(solution)/shard_map/ppermute | solution.py:298
  57.3 7.2 %collective-permute-start.7 = (f32[8,2432]{1,0:T(8,128)S(1)}, f32[8,2432]{1,0:T(8,128)S(1)}, u32[]{:S(2)}, u32[]{:S(2)}) collective-permute-start(f32[8,2432]{1,0:T(8,128)S(1)} %convert_reduce_fusion), channel_id=1, source_target_pairs={{0,128},{2,130},{128,0},{130,2},{1,129},{3,131},{129,1},{131,3},{4... | collective-permute-start | bytes 233480 | tf_op jit(solution)/shard_map/ppermute | solution.py:298
  88.2 5.4 %collective-permute-start.10 = (bf16[32,8,2304]{2,1,0:T(8,128)(2,1)S(1)}, bf16[32,8,2304]{2,1,0:T(8,128)(2,1)S(1)}, u32[]{:S(2)}, u32[]{:S(2)}) collective-permute-start(bf16[32,8,2304]{2,1,0:T(8,128)(2,1)S(1)} %all_to_all.11.own_ref), channel_id=1, source_target_pairs={{0,64},{64,0},{1,65},{65,1},{2,66},{66,2},{3,67},{67,3},{4,68},{68... | collective-permute-start | bytes 3538952 | tf_op jit(solution)/shard_map/ppermute | solution.py:289

commit v2 on v1

--- a/solution.py
+++ b/solution.py
@@ -249,6 +249,15 @@
         out_ref[d, :, pl.ds(TILES * LANES, LANES)] = tail
 
 
+def settle_step(value_ref, two_ref, one_ref, three_ref, out_ref, note_ref):
+    total = (value_ref[...] + two_ref[...]) + (one_ref[...] + three_ref[...])
+    size = TILES * LANES
+    note_ref[...] = total[:, size:]
+    piece = total[:, :size].astype(BF16)
+    for d in range(out_ref.shape[0]):
+        out_ref[d] = piece
+
+
 def place_half(slot, wide, ref, out_refs, sems):
     half = wide.shape[2]
     share = ref.shape[0] // 2
@@ -269,8 +278,8 @@
         copy.wait()
 
 
-def place_own(scale, place_ref, own_ref, total_ref, two_ref, one_ref, loss_ref, wide, sems):
-    tail = total_ref[:, pl.ds(TILES * LANES, LANES)]
+def place_own(scale, place_ref, own_ref, note_ref, two_ref, one_ref, loss_ref, wide, sems):
+    tail = note_ref[...]
     spot = lax.broadcasted_iota(jnp.int32, tail.shape, 0)
     lane = lax.broadcasted_iota(jnp.int32, tail.shape, 1)
     loss_ref[0, 0] = jnp.sum(jnp.where((spot < 3) & (lane == 0), tail, 0.0)) * scale
@@ -298,11 +307,11 @@
     return lax.ppermute(value, FAR, [(k, (k + step) % count) for k in range(count)])
 
 
-def far_sum(value):
+def far_terms(value):
     two = turn(value, 2)
     one = turn(value, 1)
     three = turn(value, 3)
-    return (value + two) + (one + three)
+    return value, two, one, three
 
 
 def placed(body, args, outs, in_specs, out_specs, aliases):
@@ -395,15 +404,20 @@
         [x_own, x_got, pre, pre_got, grad, grad_got, two],
         flops,
     )
-    total = far_sum(jnp.sum(exchange(message, PLANE).astype(F32), axis=0))
-    piece = total[:, : TILES * LANES].astype(BF16)
-    full = exchange(jnp.broadcast_to(piece[None], (2 * share,) + piece.shape), PLANE)
+    settled, note = call(
+        settle_step,
+        [shape((2 * share, 8, TILES * LANES), BF16), shape((8, LANES), F32)],
+        [],
+        list(far_terms(jnp.sum(exchange(message, PLANE).astype(F32), axis=0))),
+        0,
+    )
+    full = exchange(settled, PLANE)
     other = swap(full, "c")
     loss_scale = 1.0 / (lax.axis_size(("zh", "c", "y", "x", "za", "zb")) * channels)
     parts = [shape((9, 2, half, channels), F32)] * 2
     two, one, loss = placed(
         functools.partial(place_own, loss_scale),
-        [where, full, total],
+        [where, full, note],
         parts + [shape((1, 1), F32)],
         [SMEM, VMEM, VMEM],
         [HBM, HBM, SMEM],

time: 96.6 us -> 96.5 us (level)
    pallas_call x6 -> x7, Pallas kernels: 11 us -> 11.1 us  [call(): pl.pallas_call(body, out_shape=outs, in_specs=specs or [VMEM] * len(args)...]
where the time goes in v2:
time: 96.5 us; the launch traced here: 95.1 us
  blocking collectives  51.4 us (53%)
  starting transfers between devices  19.3 us (20%)
  Pallas kernels  14.7 us (15%)
  waiting for transfers between devices  8.76 us (9%)
    all_to_all x2, blocking collectives, exchange(): return lax.all_to_all(value, axes, 0, 0, tiled=True)  51.4 us
    pallas_call x7, Pallas kernels, call(): pl.pallas_call(body, out_shape=outs, in_specs=specs or [VMEM] * len(args)...  11.1 us
    ppermute x8, starting transfers between devices, swap(): return lax.ppermute(value, axis, [(0, 1), (1, 0)])  10.8 us
    ppermute x3, starting transfers between devices, turn(): lax.ppermute(value, FAR, [(k, (k + step) % count) for k in range(count)])  8.51 us
    ppermute x8, waiting for transfers between devices, swap(): return lax.ppermute(value, axis, [(0, 1), (1, 0)])  5.41 us
    pallas_call x2, Pallas kernels, placed(): pl.pallas_call(body, out_shape=outs, in_specs=in_specs, out_specs=out_spe...  3.61 us
    ppermute x3, waiting for transfers between devices, turn(): lax.ppermute(value, FAR, [(k, (k + step) % count) for k in range(count)])  3.35 us
  transfers between devices with their start and end apart: 11, of which 5 were waited for; matrix products, arithmetic and copies ran while one was open for 0% of the time, Pallas kernels for 5%

profile of v2, /device:TPU:97, one launch (start us, length us, event | category | flops | bytes accessed | tf_op | source)
XLA Modules:
  0.0 95.1 jit_solution(6554964908664469197)
XLA Ops:
  0.6 1.6 %shard_map.85 = (bf16[256,256]{1,0:T(8,128)(2,1)S(1)}, bf16[1024,256]{1,0:T(8,128)(2,1)S(1)}, bf16[2304,256]{1,0:T(8,128)(2,1)S(1)}) custom-call(bf16[256,512]{1,0:T(8,128)(2,1)} %bitcast.14, bf16[512,256]{1,0:T(8,128)(2,1)} %k_hbm.1, bf16[1024,256]{1,0:T(8,128)(2,1)} %bitcast.13, bf16[2304,256]{1,0:T(8,128)(2,1)} %bitcast.12), custom_call_target="tpu_custom_call" | custom-call | flops 67108864 | bytes 4063232 | tf_op jit(solution)/shard_map/pallas_call | solution.py:31
  2.3 0.0 copy-start
  2.3 4.3 %shard_map.86 = (bf16[1024,256]{1,0:T(8,128)(2,1)S(1)}, f32[1024,256]{1,0:T(8,128)S(1)}, bf16[128,1536]{1,0:T(8,128)(2,1)S(1)}, bf16[128,1536]{1,0:T(8,128)(2,1)...) custom-call(s32[1]{0:T(128)} %bitcast.place_ref, ...), custom_call_target="tpu_custom_call" | custom-call | flops 2415919104 | bytes 7208964 | tf_op jit(solution)/shard_map/pallas_call | solution.py:31
  6.6 0.8 collective-permute-start.2
  7.3 0.1 collective-permute-start.3
  7.4 4.2 %collective-permute-start = (bf16[256,256]{1,0:T(8,128)(2,1)S(1)}, bf16[256,256]{1,0:T(8,128)(2,1)S(1)}, u32[]{:S(2)}, u32[]{:S(2)}) collective-permute-start(bf16[256,256]{1,0:T(8,128)(2,1)S(1)} %get-tuple-element.38.own_ref), channel_id=1, source_target_pairs={{0,128},{128,0},{1,129},{129,1},{2,130},{130,2},{3,131},{131,3},{4... | collective-permute-start | bytes 393224 | tf_op jit(solution)/shard_map/ppermute | solution.py:298
  11.6 0.7 collective-permute-start.1
  12.3 3.6 %collective-permute-done.far_ref = bf16[256,256]{1,0:T(8,128)(2,1)S(1)} collective-permute-done((bf16[256,256]{1,0:T(8,128)(2,1)S(1)}, bf16[256,256]{1,0:T(8,128)(2,1)S(1)}, u32[]{:S(2)}, u32[]{:S(2)}) %collective-permute-start) | collective-permute-done | bytes 131104 | tf_op jit(solution)/shard_map/ppermute | solution.py:298
  16.0 0.0 collective-permute-done.1.near_ref
  16.0 0.0 collective-permute-done.2.got_turned
  16.0 0.0 collective-permute-done.3.got_turned
  16.0 1.5 %collective-permute-start.4 = (bf16[256,256]{1,0:T(8,128)(2,1)S(1)}, bf16[256,256]{1,0:T(8,128)(2,1)S(1)}, u32[]{:S(2)}, u32[]{:S(2)}) collective-permute-start(bf16[256,256]{1,0:T(8,128)(2,1)S(1)} %collective-permute-done.far_ref), channel_id=1, source_target_pairs={{0,64},{64,0},{1,65},{65,1},{2,66},{66,2},{3,67},{67,3},{4,68},{68... | collective-permute-start | bytes 393224 | tf_op jit(solution)/shard_map/ppermute | solution.py:298
  17.5 1.0 %collective-permute-done.4.both_ref = bf16[256,256]{1,0:T(8,128)(2,1)S(1)} collective-permute-done((bf16[256,256]{1,0:T(8,128)(2,1)S(1)}, bf16[256,256]{1,0:T(8,128)(2,1)S(1)}, u32[]{:S(2)}, u32[]{:S(2)}) %collective-permute-start.4) | collective-permute-done | bytes 131104 | tf_op jit(solution)/shard_map/ppermute | solution.py:298
  18.4 0.0 copy-done
  18.4 0.9 shard_map.87
  19.3 0.4 collective-permute-start.6
  19.8 1.4 %shard_map.88.own_ref = bf16[1024,256]{1,0:T(8,128)(2,1)S(1)} custom-call(bf16[3,1536,256]{2,1,0:T(8,128)(2,1)S(1)} %get-tuple-element.45.pads_ref, bf16[2304,256]{1,0:T(8,128)(2,1)S(1)} %get-tuple-element.46.k_ref, bf16[1024,256]{1,0:T(8,128)(2,1)S(1)} %get-tuple-element.47.gate_ref), custom_call_target="tpu_custom_call" | custom-call | flops 1207959552 | bytes 4587520 | tf_op jit(solution)/shard_map/pallas_call | solution.py:31
  21.2 0.2 collective-permute-start.5
  21.4 0.0 collective-permute-done.6.got_ref.other_note_ref
  21.4 1.4 %shard_map.89.two_ref = bf16[16,8,2304]{2,1,0:T(8,128)(2,1)S(1)} custom-call(bf16[128,1536]{1,0:T(8,128)(2,1)S(1)} %get-tuple-element.49.own_turned, bf16[128,1536]{1,0:T(8,128)(2,1)S(1)} %collective-permute-done.3.got_turned, bf16[3,1536,256]{2,1,0:T(8,128)(2,1)S(1)} %get-tuple-element.45.pads_ref, ...), custom_call_target="tpu_custom_call" | custom-call | flops 1207959552 | bytes 4268032 | tf_op jit(solution)/shard_map/pallas_call | solution.py:31
  22.8 0.4 collective-permute-done.5.got_ref
  23.2 1.4 %shard_map.90 = bf16[32,8,2432]{2,1,0:T(8,128)(2,1)S(1)} custom-call(bf16[128,1536]{1,0:T(8,128)(2,1)S(1)} %get-tuple-element.34.own_turned, bf16[128,1536]{1,0:T(8,128)(2,1)S(1)} %collective-permute-done.2.got_turned, bf16[1024,256]{1,0:T(8,128)(2,1)S(1)} %shard_map.88.own_ref, bf16[1024,256]{1,0:T(8,128)(2,1)S(1)} %collective-permute-done.5.got_ref, ...), custom_call_target="tpu_custom_call" | custom-call | flops 1207959552 | bytes 4734976 | tf_op jit(solution)/shard_map/pallas_call | solution.py:31
  24.6 27.9 %all_to_all.10 = bf16[32,8,2432]{2,1,0:T(8,128)(2,1)S(1)} all-to-all(bf16[32,8,2432]{2,1,0:T(8,128)(2,1)S(1)} %shard_map.90), channel_id=1, replica_groups=mesh['zh'=2,'c'=2,'y'=4,'x'=4,'za'=2,'zb'=2] {'zb','x','y'}, dimensions={0} | all-to-all | bytes 2490368 | tf_op jit(solution)/shard_map/all_to_all | solution.py:302
  52.5 0.2 convert_reduce_fusion.value_ref
  52.7 1.3 %collective-permute-start.9 = (f32[8,2432]{1,0:T(8,128)S(1)}, f32[8,2432]{1,0:T(8,128)S(1)}, u32[]{:S(2)}, u32[]{:S(2)}) collective-permute-start(f32[8,2432]{1,0:T(8,128)S(1)} %convert_reduce_fusion.value_ref), channel_id=1, source_target_pairs={{0,130},{2,0},{128,2},{130,128},{1,131},{3,1},{129,3},{131,129},{4... | collective-permute-start | bytes 233480 | tf_op jit(solution)/shard_map/ppermute | solution.py:307
  54.0 3.3 %collective-permute-start.8 = (f32[8,2432]{1,0:T(8,128)S(1)}, f32[8,2432]{1,0:T(8,128)S(1)}, u32[]{:S(2)}, u32[]{:S(2)}) collective-permute-start(f32[8,2432]{1,0:T(8,128)S(1)} %convert_reduce_fusion.value_ref), channel_id=1, source_target_pairs={{0,2},{2,128},{128,130},{130,0},{1,3},{3,129},{129,131},{131,1},{4... | collective-permute-start | bytes 233480 | tf_op jit(solution)/shard_map/ppermute | solution.py:307
  57.3 3.8 %collective-permute-start.7 = (f32[8,2432]{1,0:T(8,128)S(1)}, f32[8,2432]{1,0:T(8,128)S(1)}, u32[]{:S(2)}, u32[]{:S(2)}) collective-permute-start(f32[8,2432]{1,0:T(8,128)S(1)} %convert_reduce_fusion.value_ref), channel_id=1, source_target_pairs={{0,128},{2,130},{128,0},{130,2},{1,129},{3,131},{129,1},{131,3},{4... | collective-permute-start | bytes 233480 | tf_op jit(solution)/shard_map/ppermute | solution.py:307
  61.2 0.0 collective-permute-done.9.three_ref
  61.2 0.0 collective-permute-done.8.one_ref
  61.2 3.3 %collective-permute-done.7.two_ref = f32[8,2432]{1,0:T(8,128)S(1)} collective-permute-done((f32[8,2432]{1,0:T(8,128)S(1)}, f32[8,2432]{1,0:T(8,128)S(1)}, u32[]{:S(2)}, u32[]{:S(2)}) %collective-permute-start.7) | collective-permute-done | bytes 77856 | tf_op jit(solution)/shard_map/ppermute | solution.py:307
  64.5 0.1 shard_map.91
  64.6 23.5 %all_to_all.11.own_ref = bf16[32,8,2304]{2,1,0:T(8,128)(2,1)S(1)} all-to-all(bf16[32,8,2304]{2,1,0:T(8,128)(2,1)S(1)} %get-tuple-element.51), channel_id=1, replica_groups=mesh['zh'=2,'c'=2,'y'=4,'x'=4,'za'=2,'zb'=2] {'zb','x','y'}, dimensions={0} | all-to-all | bytes 2359296 | tf_op jit(solution)/shard_map/all_to_all | solution.py:302
  88.1 2.9 %collective-permute-start.10 = (bf16[32,8,2304]{2,1,0:T(8,128)(2,1)S(1)}, bf16[32,8,2304]{2,1,0:T(8,128)(2,1)S(1)}, u32[]{:S(2)}, u32[]{:S(2)}) collective-permute-start(bf16[32,8,2304]{2,1,0:T(8,128)(2,1)S(1)} %all_to_all.11.own_ref), channel_id=1, source_target_pairs={{0,64},{64,0},{1,65},{65,1},{2,66},{66,2},{3,67},{67,3},{4,68},{68... | collective-permute-start | bytes 3538952 | tf_op jit(solution)/shard_map/ppermute | solution.py:298
  91.1 2.1 %shard_map.92 = (f32[9,2,128,256]{3,2,1,0:T(8,128)}, f32[9,2,128,256]{3,2,1,0:T(8,128)}, f32[1,1]{1,0:T(1,128)}) custom-call(s32[1]{0:T(128)} %bitcast.place_ref, bf16[32,8,2304]{2,1,0:T(8,128)(2,1)S(1)} %all_to_all.11.own_ref, f32[8,128]{1,0:T(8,128)S(1)} %get-tuple-element.52.note_ref), custom_call_target="tpu_custom_call" | custom-call | bytes 3538944 | tf_op jit(solution)/shard_map/pallas_call | solution.py:318
  93.1 0.4 collective-permute-done.10.other_ref
  93.5 1.5 %shard_map.93 = (f32[9,2,128,256]{3,2,1,0:T(8,128)}, f32[9,2,128,256]{3,2,1,0:T(8,128)}) custom-call(s32[1]{0:T(128)} %bitcast.place_ref, bf16[32,8,2304]{2,1,0:T(8,128)(2,1)S(1)} %collective-permute-done.10.other_ref, f32[9,2,128,256]{3,2,1,0:T(8,128)} %get-tuple-element.56.two_in, ...), custom_call_target="tpu_custom_call", output_to_operand_aliasing={{0}: (2, {}), {1}: (3, {})} | custom-call | bytes 3538944 | tf_op jit(solution)/shard_map/pallas_call | solution.py:318
Async XLA Ops:
  2.3 16.2 %copy-start = (s32[1,8,128]{2,1,0:T(8,128)S(1)}, s32[1,8,128]{2,1,0:T(8,128)}, u32[]{:S(2)}) copy-start(s32[1,8,128]{2,1,0:T(8,128)} %param.8) | copy-start | bytes 12292
  6.6 9.4 %collective-permute-start.2 = (bf16[128,1536]{1,0:T(8,128)(2,1)S(1)}, bf16[128,1536]{1,0:T(8,128)(2,1)S(1)}, u32[]{:S(2)}, u32[]{:S(2)}) collective-permute-start(bf16[128,1536]{1,0:T(8,128)(2,1)S(1)} %get-tuple-element.39), channel_id=1, source_target_pairs={{0,64},{64,0},{1,65},{65,1},{2,66},{66,2},{3,67},{67,3},{4,68},{68... | collective-permute-start | bytes 1179656 | tf_op jit(solution)/shard_map/ppermute | solution.py:298
  7.3 8.7 %collective-permute-start.3 = (bf16[128,1536]{1,0:T(8,128)(2,1)S(1)}, bf16[128,1536]{1,0:T(8,128)(2,1)S(1)}, u32[]{:S(2)}, u32[]{:S(2)}) collective-permute-start(bf16[128,1536]{1,0:T(8,128)(2,1)S(1)} %get-tuple-element.40), channel_id=1, source_target_pairs={{0,64},{64,0},{1,65},{65,1},{2,66},{66,2},{3,67},{67,3},{4,68},{68... | collective-permute-start | bytes 1179656 | tf_op jit(solution)/shard_map/ppermute | solution.py:298
  7.4 8.6 %collective-permute-start = (bf16[256,256]{1,0:T(8,128)(2,1)S(1)}, bf16[256,256]{1,0:T(8,128)(2,1)S(1)}, u32[]{:S(2)}, u32[]{:S(2)}) collective-permute-start(bf16[256,256]{1,0:T(8,128)(2,1)S(1)} %get-tuple-element.38.own_ref), channel_id=1, source_target_pairs={{0,128},{128,0},{1,129},{129,1},{2,130},{130,2},{3,131},{131,3},{4... | collective-permute-start | bytes 393224 | tf_op jit(solution)/shard_map/ppermute | solution.py:298
  11.6 4.3 %collective-permute-start.1 = (bf16[256,256]{1,0:T(8,128)(2,1)S(1)}, bf16[256,256]{1,0:T(8,128)(2,1)S(1)}, u32[]{:S(2)}, u32[]{:S(2)}) collective-permute-start(bf16[256,256]{1,0:T(8,128)(2,1)S(1)} %get-tuple-element.38.own_ref), channel_id=1, source_target_pairs={{0,64},{64,0},{1,65},{65,1},{2,66},{66,2},{3,67},{67,3},{4,68},{68... | collective-permute-start | bytes 393224 | tf_op jit(solution)/shard_map/ppermute | solution.py:298
  16.0 2.4 %collective-permute-start.4 = (bf16[256,256]{1,0:T(8,128)(2,1)S(1)}, bf16[256,256]{1,0:T(8,128)(2,1)S(1)}, u32[]{:S(2)}, u32[]{:S(2)}) collective-permute-start(bf16[256,256]{1,0:T(8,128)(2,1)S(1)} %collective-permute-done.far_ref), channel_id=1, source_target_pairs={{0,64},{64,0},{1,65},{65,1},{2,66},{66,2},{3,67},{67,3},{4,68},{68... | collective-permute-start | bytes 393224 | tf_op jit(solution)/shard_map/ppermute | solution.py:298
  19.3 2.1 %collective-permute-start.6 = (bf16[1040,256]{1,0:T(8,128)(2,1)S(1)}, bf16[1040,256]{1,0:T(8,128)(2,1)S(1)}, u32[]{:S(2)}, u32[]{:S(2)}) collective-permute-start(bf16[1040,256]{1,0:T(8,128)(2,1)S(1)} %get-tuple-element.48.note_ref), channel_id=1, source_target_pairs={{0,64},{64,0},{1,65},{65,1},{2,66},{66,2},{3,67},{67,3},{4,68},{68... | collective-permute-start | bytes 1597448 | tf_op jit(solution)/shard_map/ppermute | solution.py:298
  21.2 2.0 %collective-permute-start.5 = (bf16[1024,256]{1,0:T(8,128)(2,1)S(1)}, bf16[1024,256]{1,0:T(8,128)(2,1)S(1)}, u32[]{:S(2)}, u32[]{:S(2)}) collective-permute-start(bf16[1024,256]{1,0:T(8,128)(2,1)S(1)} %shard_map.88.own_ref), channel_id=1, source_target_pairs={{0,64},{64,0},{1,65},{65,1},{2,66},{66,2},{3,67},{67,3},{4,68},{68... | collective-permute-start | bytes 1572872 | tf_op jit(solution)/shard_map/ppermute | solution.py:298
  52.7 8.5 %collective-permute-start.9 = (f32[8,2432]{1,0:T(8,128)S(1)}, f32[8,2432]{1,0:T(8,128)S(1)}, u32[]{:S(2)}, u32[]{:S(2)}) collective-permute-start(f32[8,2432]{1,0:T(8,128)S(1)} %convert_reduce_fusion.value_ref), channel_id=1, source_target_pairs={{0,130},{2,0},{128,2},{130,128},{1,131},{3,1},{129,3},{131,129},{4... | collective-permute-start | bytes 233480 | tf_op jit(solution)/shard_map/ppermute | solution.py:307
  54.0 7.2 %collective-permute-start.8 = (f32[8,2432]{1,0:T(8,128)S(1)}, f32[8,2432]{1,0:T(8,128)S(1)}, u32[]{:S(2)}, u32[]{:S(2)}) collective-permute-start(f32[8,2432]{1,0:T(8,128)S(1)} %convert_reduce_fusion.value_ref), channel_id=1, source_target_pairs={{0,2},{2,128},{128,130},{130,0},{1,3},{3,129},{129,131},{131,1},{4... | collective-permute-start | bytes 233480 | tf_op jit(solution)/shard_map/ppermute | solution.py:307
  57.3 7.2 %collective-permute-start.7 = (f32[8,2432]{1,0:T(8,128)S(1)}, f32[8,2432]{1,0:T(8,128)S(1)}, u32[]{:S(2)}, u32[]{:S(2)}) collective-permute-start(f32[8,2432]{1,0:T(8,128)S(1)} %convert_reduce_fusion.value_ref), channel_id=1, source_target_pairs={{0,128},{2,130},{128,0},{130,2},{1,129},{3,131},{129,1},{131,3},{4... | collective-permute-start | bytes 233480 | tf_op jit(solution)/shard_map/ppermute | solution.py:307
  88.1 5.4 %collective-permute-start.10 = (bf16[32,8,2304]{2,1,0:T(8,128)(2,1)S(1)}, bf16[32,8,2304]{2,1,0:T(8,128)(2,1)S(1)}, u32[]{:S(2)}, u32[]{:S(2)}) collective-permute-start(bf16[32,8,2304]{2,1,0:T(8,128)(2,1)S(1)} %all_to_all.11.own_ref), channel_id=1, source_target_pairs={{0,64},{64,0},{1,65},{65,1},{2,66},{66,2},{3,67},{67,3},{4,68},{68... | collective-permute-start | bytes 3538952 | tf_op jit(solution)/shard_map/ppermute | solution.py:298

commit v3 on v1

--- a/solution.py
+++ b/solution.py
@@ -110,11 +110,15 @@
 
 
 def forward_step(
-    rows, columns, place_ref, x_ref, one_ref, two_hbm,
-    gate_ref, pred_ref, x_own, x_give, h_own, h_give, back_ref, pads, hidden, two_ref, sem,
+    rows, columns, place_ref, x_ref, one_hbm, two_hbm,
+    gate_ref, pred_ref, x_own, x_give, h_own, h_give, back_ref, pads, hidden, one_ref, two_ref, sems,
 ):
-    load = pltpu.make_async_copy(two_hbm, two_ref, sem)
-    load.start()
+    loads = [
+        pltpu.make_async_copy(one_hbm, one_ref, sems.at[0]),
+        pltpu.make_async_copy(two_hbm, two_ref, sems.at[1]),
+    ]
+    for load in loads:
+        load.start()
 
     def of(ref):
         return lambda r: ref[pl.ds(r * columns, columns), :]
@@ -129,10 +133,11 @@
     core = place_ref[0] % 2
     channels = hidden.shape[1]
     fill_shifts(pads, of(x_ref), rows, columns, 1)
+    loads[0].wait()
     conv_rows(rows, columns, pads, one_ref, activate)
     fill_turned(core, x_own, x_give, of(x_ref), rows, columns)
     fill_shifts(pads, of(hidden), rows, columns, 1)
-    load.wait()
+    loads[1].wait()
     conv_rows(rows, columns, pads, two_ref, keep)
     fill_turned(core, h_own, h_give, of(hidden), rows, columns)
     for k in range(9):
@@ -334,15 +339,15 @@
     flops = 2 * cells * 9 * channels * channels
     weak = in_place(weak_feats.reshape(-1, in_channels))
     teacher_weight = in_place(teacher_weight)
-    operands = [in_place(strong_feats.reshape(cells, channels)), in_place(head_one.reshape(kernel))]
-    last_kernel = in_place(head_two.reshape(kernel))
+    operands = [in_place(strong_feats.reshape(cells, channels))]
+    kernels = [in_place(head_one.reshape(kernel)), in_place(head_two.reshape(kernel))]
     own, *operands = call(
         teach_step,
         [shape((weak.shape[0], channels), BF16)] + [shape(a.shape, BF16) for a in operands],
-        [pltpu.VMEM(weak.shape, BF16), pltpu.VMEM(teacher_weight.shape, BF16), pltpu.SemaphoreType.DMA((4,))],
+        [pltpu.VMEM(weak.shape, BF16), pltpu.VMEM(teacher_weight.shape, BF16), pltpu.SemaphoreType.DMA((3,))],
         [weak, teacher_weight, *operands],
         2 * weak.size * channels,
-        [HBM] * 4,
+        [HBM] * 3,
     )
     far = swap(own, "zh")
     where = (2 * lax.axis_index("zh") + lax.axis_index("c")).astype(jnp.int32).reshape(1)
@@ -353,11 +358,12 @@
             pltpu.VMEM(padded, BF16),
             pltpu.VMEM((cells, channels), BF16),
             pltpu.VMEM(kernel, BF16),
-            pltpu.SemaphoreType.DMA,
+            pltpu.VMEM(kernel, BF16),
+            pltpu.SemaphoreType.DMA((2,)),
         ],
-        [where, *operands, last_kernel],
+        [where, *operands, *kernels],
         2 * flops,
-        [SMEM, VMEM, VMEM, HBM],
+        [SMEM, VMEM, HBM, HBM],
     )
     own, x_give = lax.optimization_barrier((own, x_give))
     near, x_got, h_got = swap(own, "c"), swap(x_give, "c"), swap(h_give, "c")

time: 96.6 us -> 97.4 us (level)
  the two profiles are of different devices: /device:TPU:97 before, /device:TPU:1 now
where the time goes in v3:
time: 97.4 us; the launch traced here: 97.2 us
  blocking collectives  49 us (50%)
  starting transfers between devices  22.7 us (23%)
  Pallas kernels  15.2 us (16%)
  waiting for transfers between devices  9.27 us (10%)
    all_to_all x2, blocking collectives, exchange(): return lax.all_to_all(value, axes, 0, 0, tiled=True)  49 us
    ppermute x8, starting transfers between devices, swap(): return lax.ppermute(value, axis, [(0, 1), (1, 0)])  14.9 us
    pallas_call x6, Pallas kernels, call(): pl.pallas_call(body, out_shape=outs, in_specs=specs or [VMEM] * len(args)...  11.6 us
    ppermute x3, starting transfers between devices, turn(): lax.ppermute(value, FAR, [(k, (k + step) % count) for k in range(count)])  7.78 us
    ppermute x3, waiting for transfers between devices, turn(): lax.ppermute(value, FAR, [(k, (k + step) % count) for k in range(count)])  4.85 us
    ppermute x8, waiting for transfers between devices, swap(): return lax.ppermute(value, axis, [(0, 1), (1, 0)])  4.42 us
    pallas_call x2, Pallas kernels, placed(): pl.pallas_call(body, out_shape=outs, in_specs=in_specs, out_specs=out_spe...  3.61 us
  transfers between devices with their start and end apart: 11, of which 6 were waited for; matrix products, arithmetic and copies ran while one was open for 0% of the time, Pallas kernels for 5%

profile of v3, /device:TPU:1, one launch (start us, length us, event | category | flops | bytes accessed | tf_op | source)
XLA Modules:
  0.0 97.2 jit_solution(10812760524672161569)
XLA Ops:
  0.6 1.3 %shard_map.85 = (bf16[256,256]{1,0:T(8,128)(2,1)S(1)}, bf16[1024,256]{1,0:T(8,128)(2,1)S(1)}) custom-call(bf16[256,512]{1,0:T(8,128)(2,1)} %bitcast.13, bf16[512,256]{1,0:T(8,128)(2,1)} %k_hbm.1, bf16[1024,256]{1,0:T(8,128)(2,1)} %bitcast.12), custom_call_target="tpu_custom_call" | custom-call | flops 67108864 | bytes 1703936 | tf_op jit(solution)/shard_map/pallas_call | solution.py:31
  1.9 0.0 copy-start
  1.9 5.3 %shard_map.86 = (bf16[1024,256]{1,0:T(8,128)(2,1)S(1)}, f32[1024,256]{1,0:T(8,128)S(1)}, bf16[128,1536]{1,0:T(8,128)(2,1)S(1)}, bf16[128,1536]{1,0:T(8,128)(2,1)...) custom-call(s32[1]{0:T(128)} %bitcast.place_ref, ...), custom_call_target="tpu_custom_call" | custom-call | flops 2415919104 | bytes 7208964 | tf_op jit(solution)/shard_map/pallas_call | solution.py:31
  7.2 3.3 %collective-permute-start.2 = (bf16[128,1536]{1,0:T(8,128)(2,1)S(1)}, bf16[128,1536]{1,0:T(8,128)(2,1)S(1)}, u32[]{:S(2)}, u32[]{:S(2)}) collective-permute-start(bf16[128,1536]{1,0:T(8,128)(2,1)S(1)} %get-tuple-element.35), channel_id=1, source_target_pairs={{0,64},{64,0},{1,65},{65,1},{2,66},{66,2},{3,67},{67,3},{4,68},{68... | collective-permute-start | bytes 1179656 | tf_op jit(solution)/shard_map/ppermute | solution.py:294
  10.5 0.1 collective-permute-start.3
  10.6 5.2 %collective-permute-start = (bf16[256,256]{1,0:T(8,128)(2,1)S(1)}, bf16[256,256]{1,0:T(8,128)(2,1)S(1)}, u32[]{:S(2)}, u32[]{:S(2)}) collective-permute-start(bf16[256,256]{1,0:T(8,128)(2,1)S(1)} %get-tuple-element.34.own_ref), channel_id=1, source_target_pairs={{0,128},{128,0},{1,129},{129,1},{2,130},{130,2},{3,131},{131,3},{4... | collective-permute-start | bytes 393224 | tf_op jit(solution)/shard_map/ppermute | solution.py:294
  15.8 0.7 collective-permute-start.1
  16.5 2.7 %collective-permute-done.far_ref = bf16[256,256]{1,0:T(8,128)(2,1)S(1)} collective-permute-done((bf16[256,256]{1,0:T(8,128)(2,1)S(1)}, bf16[256,256]{1,0:T(8,128)(2,1)S(1)}, u32[]{:S(2)}, u32[]{:S(2)}) %collective-permute-start) | collective-permute-done | bytes 131104 | tf_op jit(solution)/shard_map/ppermute | solution.py:294
  19.2 0.0 collective-permute-done.1.near_ref
  19.2 0.0 collective-permute-done.2.got_turned
  19.2 0.0 collective-permute-done.3.got_turned
  19.2 1.5 %collective-permute-start.4 = (bf16[256,256]{1,0:T(8,128)(2,1)S(1)}, bf16[256,256]{1,0:T(8,128)(2,1)S(1)}, u32[]{:S(2)}, u32[]{:S(2)}) collective-permute-start(bf16[256,256]{1,0:T(8,128)(2,1)S(1)} %collective-permute-done.far_ref), channel_id=1, source_target_pairs={{0,64},{64,0},{1,65},{65,1},{2,66},{66,2},{3,67},{67,3},{4,68},{68... | collective-permute-start | bytes 393224 | tf_op jit(solution)/shard_map/ppermute | solution.py:294
  20.6 1.0 %collective-permute-done.4.both_ref = bf16[256,256]{1,0:T(8,128)(2,1)S(1)} collective-permute-done((bf16[256,256]{1,0:T(8,128)(2,1)S(1)}, bf16[256,256]{1,0:T(8,128)(2,1)S(1)}, u32[]{:S(2)}, u32[]{:S(2)}) %collective-permute-start.4) | collective-permute-done | bytes 131104 | tf_op jit(solution)/shard_map/ppermute | solution.py:294
  21.6 0.0 copy-done
  21.6 0.8 shard_map.87
  22.5 0.4 collective-permute-start.6
  22.9 1.4 %shard_map.88.own_ref = bf16[1024,256]{1,0:T(8,128)(2,1)S(1)} custom-call(bf16[3,1536,256]{2,1,0:T(8,128)(2,1)S(1)} %get-tuple-element.41.pads_ref, bf16[2304,256]{1,0:T(8,128)(2,1)S(1)} %get-tuple-element.42.k_ref, bf16[1024,256]{1,0:T(8,128)(2,1)S(1)} %get-tuple-element.43.gate_ref), custom_call_target="tpu_custom_call" | custom-call | flops 1207959552 | bytes 4587520 | tf_op jit(solution)/shard_map/pallas_call | solution.py:31
  24.3 0.2 collective-permute-start.5
  24.5 0.0 collective-permute-done.6.got_ref.other_note_ref
  24.6 1.4 %shard_map.89.two_ref = bf16[16,8,2304]{2,1,0:T(8,128)(2,1)S(1)} custom-call(bf16[128,1536]{1,0:T(8,128)(2,1)S(1)} %get-tuple-element.45.own_turned, bf16[128,1536]{1,0:T(8,128)(2,1)S(1)} %collective-permute-done.3.got_turned, bf16[3,1536,256]{2,1,0:T(8,128)(2,1)S(1)} %get-tuple-element.41.pads_ref, ...), custom_call_target="tpu_custom_call" | custom-call | flops 1207959552 | bytes 4268032 | tf_op jit(solution)/shard_map/pallas_call | solution.py:31
  25.9 0.4 collective-permute-done.5.got_ref
  26.3 1.4 %shard_map.90 = bf16[32,8,2432]{2,1,0:T(8,128)(2,1)S(1)} custom-call(bf16[128,1536]{1,0:T(8,128)(2,1)S(1)} %get-tuple-element.30.own_turned, bf16[128,1536]{1,0:T(8,128)(2,1)S(1)} %collective-permute-done.2.got_turned, bf16[1024,256]{1,0:T(8,128)(2,1)S(1)} %shard_map.88.own_ref, bf16[1024,256]{1,0:T(8,128)(2,1)S(1)} %collective-permute-done.5.got_ref, ...), custom_call_target="tpu_custom_call" | custom-call | flops 1207959552 | bytes 4734976 | tf_op jit(solution)/shard_map/pallas_call | solution.py:31
  27.8 28.6 %all_to_all.10 = bf16[32,8,2432]{2,1,0:T(8,128)(2,1)S(1)} all-to-all(bf16[32,8,2432]{2,1,0:T(8,128)(2,1)S(1)} %shard_map.90), channel_id=1, replica_groups=mesh['zh'=2,'c'=2,'y'=4,'x'=4,'za'=2,'zb'=2] {'zb','x','y'}, dimensions={0} | all-to-all | bytes 2490368 | tf_op jit(solution)/shard_map/all_to_all | solution.py:298
  56.4 0.2 convert_reduce_fusion
  56.6 4.0 %collective-permute-start.9 = (f32[8,2432]{1,0:T(8,128)S(1)}, f32[8,2432]{1,0:T(8,128)S(1)}, u32[]{:S(2)}, u32[]{:S(2)}) collective-permute-start(f32[8,2432]{1,0:T(8,128)S(1)} %convert_reduce_fusion), channel_id=1, source_target_pairs={{0,130},{2,0},{128,2},{130,128},{1,131},{3,1},{129,3},{131,129},{4... | collective-permute-start | bytes 233480 | tf_op jit(solution)/shard_map/ppermute | solution.py:303
  60.6 0.0 collective-permute-start.8
  60.6 3.8 %collective-permute-start.7 = (f32[8,2432]{1,0:T(8,128)S(1)}, f32[8,2432]{1,0:T(8,128)S(1)}, u32[]{:S(2)}, u32[]{:S(2)}) collective-permute-start(f32[8,2432]{1,0:T(8,128)S(1)} %convert_reduce_fusion), channel_id=1, source_target_pairs={{0,128},{2,130},{128,0},{130,2},{1,129},{3,131},{129,1},{131,3},{4... | collective-permute-start | bytes 233480 | tf_op jit(solution)/shard_map/ppermute | solution.py:303
  64.4 0.0 collective-permute-done.9
  64.4 1.8 %collective-permute-done.8 = f32[8,2432]{1,0:T(8,128)S(1)} collective-permute-done((f32[8,2432]{1,0:T(8,128)S(1)}, f32[8,2432]{1,0:T(8,128)S(1)}, u32[]{:S(2)}, u32[]{:S(2)}) %collective-permute-start.8) | collective-permute-done | bytes 77856 | tf_op jit(solution)/shard_map/ppermute | solution.py:303
  66.2 3.1 %collective-permute-done.7 = f32[8,2432]{1,0:T(8,128)S(1)} collective-permute-done((f32[8,2432]{1,0:T(8,128)S(1)}, f32[8,2432]{1,0:T(8,128)S(1)}, u32[]{:S(2)}, u32[]{:S(2)}) %collective-permute-start.7) | collective-permute-done | bytes 77856 | tf_op jit(solution)/shard_map/ppermute | solution.py:303
  69.3 0.1 broadcast_in_dim.2
  69.3 20.3 %all_to_all.11.own_ref = bf16[32,8,2304]{2,1,0:T(8,128)(2,1)S(1)} all-to-all(bf16[32,8,2304]{2,1,0:T(8,128)(2,1)S(1)} %broadcast_in_dim.2), channel_id=1, replica_groups=mesh['zh'=2,'c'=2,'y'=4,'x'=4,'za'=2,'zb'=2] {'zb','x','y'}, dimensions={0} | all-to-all | bytes 2359296 | tf_op jit(solution)/shard_map/all_to_all | solution.py:298
  89.7 3.5 %collective-permute-start.10 = (bf16[32,8,2304]{2,1,0:T(8,128)(2,1)S(1)}, bf16[32,8,2304]{2,1,0:T(8,128)(2,1)S(1)}, u32[]{:S(2)}, u32[]{:S(2)}) collective-permute-start(bf16[32,8,2304]{2,1,0:T(8,128)(2,1)S(1)} %all_to_all.11.own_ref), channel_id=1, source_target_pairs={{0,64},{64,0},{1,65},{65,1},{2,66},{66,2},{3,67},{67,3},{4,68},{68... | collective-permute-start | bytes 3538952 | tf_op jit(solution)/shard_map/ppermute | solution.py:294
  93.1 2.1 %shard_map.91 = (f32[9,2,128,256]{3,2,1,0:T(8,128)}, f32[9,2,128,256]{3,2,1,0:T(8,128)}, f32[1,1]{1,0:T(1,128)}) custom-call(s32[1]{0:T(128)} %bitcast.place_ref, bf16[32,8,2304]{2,1,0:T(8,128)(2,1)S(1)} %all_to_all.11.own_ref, f32[8,2432]{1,0:T(8,128)S(1)} %add_add_fusion.total_ref), custom_call_target="tpu_custom_call" | custom-call | bytes 3538944 | tf_op jit(solution)/shard_map/pallas_call | solution.py:314
  95.2 0.4 collective-permute-done.10.other_ref
  95.6 1.5 %shard_map.92 = (f32[9,2,128,256]{3,2,1,0:T(8,128)}, f32[9,2,128,256]{3,2,1,0:T(8,128)}) custom-call(s32[1]{0:T(128)} %bitcast.place_ref, bf16[32,8,2304]{2,1,0:T(8,128)(2,1)S(1)} %collective-permute-done.10.other_ref, f32[9,2,128,256]{3,2,1,0:T(8,128)} %get-tuple-element.50.two_in, ...), custom_call_target="tpu_custom_call", output_to_operand_aliasing={{0}: (2, {}), {1}: (3, {})} | custom-call | bytes 3538944 | tf_op jit(solution)/shard_map/pallas_call | solution.py:314
  (2 shorter events, 0.0 us)
Async XLA Ops:
  1.9 19.7 %copy-start = (s32[1,8,128]{2,1,0:T(8,128)S(1)}, s32[1,8,128]{2,1,0:T(8,128)}, u32[]{:S(2)}) copy-start(s32[1,8,128]{2,1,0:T(8,128)} %param.8) | copy-start | bytes 12292
  7.2 11.9 %collective-permute-start.2 = (bf16[128,1536]{1,0:T(8,128)(2,1)S(1)}, bf16[128,1536]{1,0:T(8,128)(2,1)S(1)}, u32[]{:S(2)}, u32[]{:S(2)}) collective-permute-start(bf16[128,1536]{1,0:T(8,128)(2,1)S(1)} %get-tuple-element.35), channel_id=1, source_target_pairs={{0,64},{64,0},{1,65},{65,1},{2,66},{66,2},{3,67},{67,3},{4,68},{68... | collective-permute-start | bytes 1179656 | tf_op jit(solution)/shard_map/ppermute | solution.py:294
  10.5 8.7 %collective-permute-start.3 = (bf16[128,1536]{1,0:T(8,128)(2,1)S(1)}, bf16[128,1536]{1,0:T(8,128)(2,1)S(1)}, u32[]{:S(2)}, u32[]{:S(2)}) collective-permute-start(bf16[128,1536]{1,0:T(8,128)(2,1)S(1)} %get-tuple-element.36), channel_id=1, source_target_pairs={{0,64},{64,0},{1,65},{65,1},{2,66},{66,2},{3,67},{67,3},{4,68},{68... | collective-permute-start | bytes 1179656 | tf_op jit(solution)/shard_map/ppermute | solution.py:294
  10.6 8.6 %collective-permute-start = (bf16[256,256]{1,0:T(8,128)(2,1)S(1)}, bf16[256,256]{1,0:T(8,128)(2,1)S(1)}, u32[]{:S(2)}, u32[]{:S(2)}) collective-permute-start(bf16[256,256]{1,0:T(8,128)(2,1)S(1)} %get-tuple-element.34.own_ref), channel_id=1, source_target_pairs={{0,128},{128,0},{1,129},{129,1},{2,130},{130,2},{3,131},{131,3},{4... | collective-permute-start | bytes 393224 | tf_op jit(solution)/shard_map/ppermute | solution.py:294
  15.8 3.3 %collective-permute-start.1 = (bf16[256,256]{1,0:T(8,128)(2,1)S(1)}, bf16[256,256]{1,0:T(8,128)(2,1)S(1)}, u32[]{:S(2)}, u32[]{:S(2)}) collective-permute-start(bf16[256,256]{1,0:T(8,128)(2,1)S(1)} %get-tuple-element.34.own_ref), channel_id=1, source_target_pairs={{0,64},{64,0},{1,65},{65,1},{2,66},{66,2},{3,67},{67,3},{4,68},{68... | collective-permute-start | bytes 393224 | tf_op jit(solution)/shard_map/ppermute | solution.py:294
  19.2 2.4 %collective-permute-start.4 = (bf16[256,256]{1,0:T(8,128)(2,1)S(1)}, bf16[256,256]{1,0:T(8,128)(2,1)S(1)}, u32[]{:S(2)}, u32[]{:S(2)}) collective-permute-start(bf16[256,256]{1,0:T(8,128)(2,1)S(1)} %collective-permute-done.far_ref), channel_id=1, source_target_pairs={{0,64},{64,0},{1,65},{65,1},{2,66},{66,2},{3,67},{67,3},{4,68},{68... | collective-permute-start | bytes 393224 | tf_op jit(solution)/shard_map/ppermute | solution.py:294
  22.5 2.1 %collective-permute-start.6 = (bf16[1040,256]{1,0:T(8,128)(2,1)S(1)}, bf16[1040,256]{1,0:T(8,128)(2,1)S(1)}, u32[]{:S(2)}, u32[]{:S(2)}) collective-permute-start(bf16[1040,256]{1,0:T(8,128)(2,1)S(1)} %get-tuple-element.44.note_ref), channel_id=1, source_target_pairs={{0,64},{64,0},{1,65},{65,1},{2,66},{66,2},{3,67},{67,3},{4,68},{68... | collective-permute-start | bytes 1597448 | tf_op jit(solution)/shard_map/ppermute | solution.py:294
  24.3 2.0 %collective-permute-start.5 = (bf16[1024,256]{1,0:T(8,128)(2,1)S(1)}, bf16[1024,256]{1,0:T(8,128)(2,1)S(1)}, u32[]{:S(2)}, u32[]{:S(2)}) collective-permute-start(bf16[1024,256]{1,0:T(8,128)(2,1)S(1)} %shard_map.88.own_ref), channel_id=1, source_target_pairs={{0,64},{64,0},{1,65},{65,1},{2,66},{66,2},{3,67},{67,3},{4,68},{68... | collective-permute-start | bytes 1572872 | tf_op jit(solution)/shard_map/ppermute | solution.py:294
  56.6 7.8 %collective-permute-start.9 = (f32[8,2432]{1,0:T(8,128)S(1)}, f32[8,2432]{1,0:T(8,128)S(1)}, u32[]{:S(2)}, u32[]{:S(2)}) collective-permute-start(f32[8,2432]{1,0:T(8,128)S(1)} %convert_reduce_fusion), channel_id=1, source_target_pairs={{0,130},{2,0},{128,2},{130,128},{1,131},{3,1},{129,3},{131,129},{4... | collective-permute-start | bytes 233480 | tf_op jit(solution)/shard_map/ppermute | solution.py:303
  60.6 5.6 %collective-permute-start.8 = (f32[8,2432]{1,0:T(8,128)S(1)}, f32[8,2432]{1,0:T(8,128)S(1)}, u32[]{:S(2)}, u32[]{:S(2)}) collective-permute-start(f32[8,2432]{1,0:T(8,128)S(1)} %convert_reduce_fusion), channel_id=1, source_target_pairs={{0,2},{2,128},{128,130},{130,0},{1,3},{3,129},{129,131},{131,1},{4... | collective-permute-start | bytes 233480 | tf_op jit(solution)/shard_map/ppermute | solution.py:303
  60.6 8.7 %collective-permute-start.7 = (f32[8,2432]{1,0:T(8,128)S(1)}, f32[8,2432]{1,0:T(8,128)S(1)}, u32[]{:S(2)}, u32[]{:S(2)}) collective-permute-start(f32[8,2432]{1,0:T(8,128)S(1)} %convert_reduce_fusion), channel_id=1, source_target_pairs={{0,128},{2,130},{128,0},{130,2},{1,129},{3,131},{129,1},{131,3},{4... | collective-permute-start | bytes 233480 | tf_op jit(solution)/shard_map/ppermute | solution.py:303
  89.7 5.9 %collective-permute-start.10 = (bf16[32,8,2304]{2,1,0:T(8,128)(2,1)S(1)}, bf16[32,8,2304]{2,1,0:T(8,128)(2,1)S(1)}, u32[]{:S(2)}, u32[]{:S(2)}) collective-permute-start(bf16[32,8,2304]{2,1,0:T(8,128)(2,1)S(1)} %all_to_all.11.own_ref), channel_id=1, source_target_pairs={{0,64},{64,0},{1,65},{65,1},{2,66},{66,2},{3,67},{67,3},{4,68},{68... | collective-permute-start | bytes 3538952 | tf_op jit(solution)/shard_map/ppermute | solution.py:294
